TPU v7x, 256 devices: a whole 4x4x8 slice. The times are simulated.
256 devices in a mesh: seq: 64 (over z, y, core), head: 4 (over x).
Axes of the slice: x: 4, y: 4, z: 8, core: 2. Of those that a mesh axis runs over, the one named last changes fastest.
Arguments:
- query_in: bfloat16 [16384, 4096], P('seq', 'head'), may hold values from -6 to 6
- key_in: bfloat16 [16384, 4096], P('seq', 'head'), may hold values from -6 to 6
- value_in: bfloat16 [16384, 4096], P('seq', 'head')
- out_grad: bfloat16 [16384, 4096], P('seq', 'head'), may hold values from -6 to 6
- norm_gain: float32 [4096], P('head'), may hold values from 0.5 to 1.5
- doc_ids: int32 [16384], P('seq'), may hold values from 0 to 35, as said below
- start_group: int32 [64], replicated, may hold values from 0 to 62, as said below
Outputs:
- normed: bfloat16 [16384, 4096], P('seq', 'head')
- grad_query: bfloat16 [16384, 4096], P('seq', 'head')
- grad_key: bfloat16 [16384, 4096], P('seq', 'head')
- grad_value: bfloat16 [16384, 4096], P('seq', 'head')
Inputs may be any that keep to these rules, and one draw needn't show every extreme that they name: `doc_ids`: 0 at the first token, never falling, one more at each document start. `start_group`: entry c is the block in which the document holding block c's first token begins; it agrees with doc_ids.
All inputs are finite; a program needn't handle non-finite values.
Results may differ from a plain program's by a relative error of at most 0.0058.
Values may be sent and summed in bfloat16 or wider, within the bound.
A program may use at most 128 MiB of HBM per device.

v0:
```python
import jax
import jax.numpy as jnp
from jax import lax
from jax.sharding import PartitionSpec as P

H = 32
HD = 128


epsilon = 1e-06


def prefix(x, axis, combine, identity, reverse):
    length, mine = (lax.axis_size(axis), lax.axis_index(axis))
    everything = jax.tree.map(lambda part: lax.all_gather(part, axis), x)
    start = jax.tree.map(
        lambda part, zero: jnp.broadcast_to(jnp.asarray(zero, part.dtype), part.shape), x, identity
    )

    def lap(k, before):
        at = length - 1 - k if reverse else k
        reached = at > mine if reverse else at < mine
        new = combine(before, jax.tree.map(lambda part: part[at], everything))
        return jax.tree.map(lambda a, b: jnp.where(reached, a, b), new, before)

    return lax.fori_loop(0, length, lap, start)


def segment_join(earlier, later):
    return (
        jnp.maximum(earlier[0], later[0]),
        jnp.where(later[0] > 0.5, later[1], earlier[1] + later[1]),
    )


def local(query_in, key_in, value_in, out_grad, norm_gain, doc_ids, start_group):
    length = query_in.shape[0]
    heads_here = query_in.shape[1] // HD
    width = H * HD
    groups = lax.axis_size("seq")
    group_index = lax.axis_index("seq")
    query_h = query_in.reshape(length, heads_here, HD)
    key_h = key_in.reshape(length, heads_here, HD)
    value_h = value_in.reshape(length, heads_here, HD)
    grad_h = out_grad.reshape(length, heads_here, HD)
    gain_heads = norm_gain.reshape(heads_here, HD)
    first_doc = doc_ids == doc_ids[0]
    last_doc = doc_ids == doc_ids[length - 1]
    first_f = first_doc.astype(jnp.float32)[:, None, None]
    last_f = last_doc.astype(jnp.float32)[:, None, None]
    causal = jnp.arange(length)[:, None] >= jnp.arange(length)[None, :]
    same_doc = causal & (doc_ids[:, None] == doc_ids[None, :])
    local_change = jnp.any(doc_ids[1:] != doc_ids[:-1])
    own_start = start_group[group_index]
    next_start = start_group[jnp.minimum(group_index + 1, groups - 1)]
    tail_state = jnp.einsum(
        "tha,thb->hab",
        key_h * last_doc.astype(jnp.bfloat16)[:, None, None],
        value_h,
        preferred_element_type=jnp.float32,
    )
    restart = jnp.where(local_change | (own_start == group_index), 1.0, 0.0).astype(jnp.float32)
    scanned = prefix(
        (restart, tail_state),
        "seq",
        segment_join,
        (jnp.zeros((), jnp.float32), jnp.zeros_like(tail_state)),
        False,
    )
    carry_b = jnp.where(own_start == group_index, 0.0, scanned[1]).astype(jnp.bfloat16)
    scores = jnp.einsum("tha,uha->htu", query_h, key_h, preferred_element_type=jnp.float32)
    weights = jnp.where(same_doc[None], scores, 0.0).astype(jnp.bfloat16)
    attended = jnp.einsum("htu,uhb->thb", weights, value_h, preferred_element_type=jnp.float32)
    attended = attended + first_f * jnp.einsum(
        "tha,hab->thb", query_h, carry_b, preferred_element_type=jnp.float32
    )
    square_part = jnp.sum(attended * attended, axis=(1, 2))
    cross_part = jnp.sum(gain_heads * grad_h * attended, axis=(1, 2))
    square_total = lax.psum(square_part, "head")
    inverse_rms = lax.rsqrt(square_total / width + epsilon)
    normed = (attended * inverse_rms[:, None, None] * gain_heads).astype(jnp.bfloat16)
    cross_total = lax.psum(cross_part, "head")
    grad_attended = (
        inverse_rms[:, None, None] * gain_heads * grad_h
        - (inverse_rms**3 * cross_total / width)[:, None, None] * attended
    ).astype(jnp.bfloat16)
    head_state = jnp.einsum(
        "tha,thb->hab",
        query_h * first_doc.astype(jnp.bfloat16)[:, None, None],
        grad_attended,
        preferred_element_type=jnp.float32,
    )
    closing = jnp.where(local_change | (next_start == group_index + 1), 1.0, 0.0).astype(
        jnp.float32
    )
    scanned_back = prefix(
        (closing, head_state),
        "seq",
        segment_join,
        (jnp.zeros((), jnp.float32), jnp.zeros_like(head_state)),
        True,
    )
    back_b = jnp.where(next_start == group_index + 1, 0.0, scanned_back[1]).astype(jnp.bfloat16)
    grad_scores = jnp.where(
        same_doc[None],
        jnp.einsum("tha,uha->htu", grad_attended, value_h, preferred_element_type=jnp.float32),
        0.0,
    ).astype(jnp.bfloat16)
    grad_query = jnp.einsum("htu,uha->tha", grad_scores, key_h, preferred_element_type=jnp.float32)
    grad_query = grad_query + first_f * jnp.einsum(
        "thb,hab->tha", grad_attended, carry_b, preferred_element_type=jnp.float32
    )
    grad_key = jnp.einsum("htu,tha->uha", grad_scores, query_h, preferred_element_type=jnp.float32)
    grad_key = grad_key + last_f * jnp.einsum(
        "uhb,hab->uha", value_h, back_b, preferred_element_type=jnp.float32
    )
    grad_value = jnp.einsum(
        "htu,thb->uhb", weights, grad_attended, preferred_element_type=jnp.float32
    )
    grad_value = grad_value + last_f * jnp.einsum(
        "uha,hab->uhb", key_h, back_b, preferred_element_type=jnp.float32
    )
    shape = (length, heads_here * HD)
    return (
        normed.reshape(shape),
        grad_query.astype(jnp.bfloat16).reshape(shape),
        grad_key.astype(jnp.bfloat16).reshape(shape),
        grad_value.astype(jnp.bfloat16).reshape(shape),
    )


def solution(mesh):
    placed = (
        P("seq", "head"),
        P("seq", "head"),
        P("seq", "head"),
        P("seq", "head"),
        P("head"),
        P("seq"),
        P(),
    )
    return jax.shard_map(
        local,
        mesh=mesh,
        in_specs=placed,
        out_specs=(P("seq", "head"), P("seq", "head"), P("seq", "head"), P("seq", "head")),
        check_vma=False,
    )
```

profile of v0, /device:TPU:1, one launch (start us, length us, event | category | flops | bytes accessed | tf_op | source)
XLA Modules:
  0.0 652.1 jit_solution(11175044496091271575)
XLA Ops:
  7.2 1.3 fusion.41
  10.1 1.3 fusion.37
  17.0 1.4 copy.40
  20.7 132.4 %all-reduce.2 = (f32[64]{0:T(128)S(1)}, f32[64]{0:T(128)S(1)}) all-reduce(f32[64]{0:T(128)S(1)} %dynamic-update-slice, f32[64]{0:T(128)S(1)} %dynamic-update-slice.1), channel_id=1, replica_groups=mesh['seq'=64,'head'=4] {'seq'}, use_global_device_ids=true, to_apply=%add | all-reduce | flops 128 | bytes 1024
  154.6 1.5 convolution_bitcast_fusion.2
  156.1 3.3 all-gather.5.cloned.1.call-done
  159.4 164.2 %while.30 = (s32[]{:T(128)}, f32[8,128,128]{2,1,0:T(8,128)S(1)}, s32[]{:T(128)}, f32[64]{0:T(128)S(1)}, f32[64,8,128,128]{3,2,1,0:T(8,128)}, /*index=5*/s32[]{:T(128)}, s32[]{:T(128)}, f32[1]{0:T(128)}) while((s32[]{:T(128)}, f32[8,128,128]{2,1,0:T(8,128)S(1)}, s32[]{:T(128)}, f32[64]{0:T(128)S(1)}, f32[64,8,128,128]{3,2,1,0:T(8,128)}, ...), condition=%wide.region_2.3_spmd.clone, body=%wide.region_1.2_spmd.clone.sunk | while | flops 524293 | bytes 1573003 | solution.py:26
  160.7 1.3 fusion.64
  163.2 1.3 fusion.64
  165.8 1.3 fusion.64
  168.4 1.3 fusion.64
  170.9 1.3 fusion.64
  176.1 1.3 fusion.64
  178.6 1.3 fusion.64
  181.2 1.3 fusion.64
  183.8 1.3 fusion.64
  323.6 2.7 multiply_reduce_fusion
  326.3 8.4 %all-reduce.3 = (f32[256]{0:T(256)S(1)}, f32[256]{0:T(256)S(1)}) all-reduce(f32[256]{0:T(256)S(1)} %get-tuple-element.277, f32[256]{0:T(256)S(1)} %get-tuple-element.276), channel_id=1, replica_groups=mesh['seq'=64,'head'=4] {'head'}, use_global_device_ids=true, to_apply=%region_4.5 | all-reduce | flops 512 | bytes 4096 | tf_op jit(solution)/shard_map/psum | solution.py:79
  334.7 2.3 subtract_convert_fusion
  341.3 2.1 copy.52
  343.4 1.3 fusion.43
  345.0 131.7 %all-gather.7.cloned.1.call-done = f32[512,128,128]{2,1,0:T(8,128)} async-done(((f32[8,128,128]{2,1,0:T(8,128)}), f32[512,128,128]{2,1,0:T(8,128)}) %all-gather.7.cloned.1.call-update) | async-done | bytes 33554448 | tf_op jit(solution)/shard_map/all_gather | solution.py:15
  476.7 164.7 %while.31 = (s32[]{:T(128)}, f32[8,128,128]{2,1,0:T(8,128)S(1)}, s32[]{:T(128)}, f32[64]{0:T(128)S(1)}, f32[64,8,128,128]{3,2,1,0:T(8,128)}, /*index=5*/s32[]{:T(128)}, s32[]{:T(128)}, s32[]{:T(128)}, s32[]{:T(128)}, f32[1]{0:T(128)}) while((s32[]{:T(128)}, f32[8,128,128]{2,1,0:T(8,128)S(1)}, s32[]{:T(128)}, f32[64]{0:T(128)S(1)}, ...), condition=%wide.region_8.9_spmd.clone, body=%wide.region_7.8_spmd.clone.sunk | while | flops 524297 | bytes 1573065 | solution.py:26
  641.4 1.6 fusion.11
  (310 shorter events, 245.1 us)
Async XLA Ops:
  7.2 4.3 copy-start
  7.2 2.9 copy-start.13
  7.2 152.2 %all-gather.5.cloned.1.call-start = ((), (), s32[]{:S(2)}) async-start(), calls=%async_computation | async-start | bytes 34078720 | tf_op jit(solution)/shard_map/all_gather | solution.py:15
  8.6 4.1 copy-start.15
  8.6 8.2 %copy-start.12 = (bf16[256,1024]{1,0:T(8,128)(2,1)S(1)}, bf16[256,1024]{1,0:T(8,128)(2,1)}, u32[]{:S(2)}) copy-start(bf16[256,1024]{1,0:T(8,128)(2,1)} %param.11) | copy-start | bytes 1572868
  10.1 6.0 copy-start.3
  11.5 6.9 %copy-start.16 = (u32[256]{0:T(256)S(1)}, u32[256]{0:T(256)}, u32[]{:S(2)}) copy-start(u32[256]{0:T(256)} %constant.110) | copy-start | bytes 3076
  11.5 141.7 %copy-start.9 = (bf16[256,1024]{1,0:T(8,128)(2,1)S(1)}, bf16[256,1024]{1,0:T(8,128)(2,1)}, u32[]{:S(2)}) copy-start(bf16[256,1024]{1,0:T(8,128)(2,1)} %param.12) | copy-start | bytes 1572868
  12.6 464.1 %all-gather.7.cloned.1.call-start = ((), (), s32[]{:S(2)}) async-start(), calls=%async_computation.1 | async-start | bytes 34078720 | tf_op jit(solution)/shard_map/all_gather | solution.py:15
  17.0 320.1 %copy-start.1 = (bf16[256,1024]{0,1:T(8,128)(2,1)}, bf16[256,1024]{0,1:T(8,128)(2,1)S(1)}, u32[]{:S(2)}) copy-start(bf16[256,1024]{0,1:T(8,128)(2,1)S(1)} %copy.60) | copy-start | bytes 1572868
  153.6 1.0 copy-start.5
  159.4 164.2 %copy-start.14 = (f32[1024]{0:T(1024)S(1)}, f32[1024]{0:T(1024)}, u32[]{:S(2)}) copy-start(f32[1024]{0:T(1024)} %param.15) | copy-start | bytes 12292
  337.0 1.1 copy-start.11
  338.1 1.5 copy-start.4
  339.7 1.6 copy-start.7
  340.2 3.2 copy-start.6
  341.3 3.4 copy-start.2
  343.4 1.3 copy-start.8
  476.7 164.7 %copy-start.10 = (bf16[256,1024]{1,0:T(8,128)(2,1)S(1)}, bf16[256,1024]{1,0:T(8,128)(2,1)}, u32[]{:S(2)}) copy-start(bf16[256,1024]{1,0:T(8,128)(2,1)} %param.12) | copy-start | bytes 1572868
Sparse Core Ops, SparseCore 0:
  12.7 146.6 all-gather.4
  338.3 138.3 all-gather.6
where the time goes:
time: 660 us; the launch traced here: 652 us
  other arithmetic  171 us (26%)
  blocking collectives  141 us (21%)
  waiting for transfers between devices  135 us (20%)
  local copies, waits for them, and re-layouts  88.8 us (13%)
  loops' own time  87.1 us (13%)
  between operations  17 us (3%)
  matrix products  12.4 us (2%)
    select_n x128, other arithmetic, lap(): return jax.tree.map(lambda a, b: jnp.where(reached, a, b), new, before)  167 us
    all_gather x2, waiting for transfers between devices, prefix(): everything = jax.tree.map(lambda part: lax.all_gather(part, axis), x)  135 us
    unnamed x1, blocking collectives  132 us
    another operation x2, loops' own time, prefix(): return lax.fori_loop(0, length, lap, start)  87.1 us
    dynamic_slice x128, local copies, waits for them, and re-layouts, lap(): new = combine(before, jax.tree.map(lambda part: part[at], everything))  75.2 us
  transfers between devices with their start and end apart: 2, of which 2 were waited for; matrix products, arithmetic and copies ran while one was open for 2% of the time, Pallas kernels for 0%

commit v1 on v0

v1 whole, which is shorter than its diff:
```python
import functools

import jax
import jax.numpy as jnp
from jax import lax
from jax.experimental import pallas as pl
from jax.experimental.pallas import tpu as pltpu
from jax.sharding import PartitionSpec as P

HD = 128
EPSILON = 1e-06
CHUNKS = 2
MESH = pl.DeviceIdType.MESH
f32, bf16 = jnp.float32, jnp.bfloat16


def dot(a, b, contract):
    return lax.dot_general(a, b, (contract, ((), ())), preferred_element_type=f32)


NN = ((1,), (0,))
NT = ((1,), (1,))
TN = ((0,), (0,))


def kernel(
    planes, heads, spread, width,
    sg_ref, doc_ref, q_ref, k_ref, v_ref, g_ref, gain_ref,
    normed_ref, gq_ref, gk_ref, gv_ref,
    same_ref, first_ref, last_ref, inv_ref, coef_ref,
    weights_ref, att_ref, ga_ref, gk_acc, gv_acc,
    tail_out, tail_in, pre_ref, agg_out, agg_in, carry_out, carry_in,
    head_out, head_in, suf_ref, bagg_out, bagg_in, back_out, back_in,
    sums_out, sums_in,
    plane_send, plane_recv, z_send, z_recv, x_send, x_recv,
):
    seq, col = lax.axis_index("seq"), lax.axis_index("head")
    z, p = lax.div(seq, heads), lax.rem(seq, heads)
    tokens = q_ref.shape[0]
    rows = HD // CHUNKS
    base = z * heads

    def plane_peer(d):
        return lax.rem(p + d, heads)

    barrier = pltpu.get_barrier_semaphore()
    for d in range(1, heads):
        pl.semaphore_signal(barrier, inc=1, device_id=(base + plane_peer(d), col), device_id_type=MESH)
    for d in range(1, planes):
        pl.semaphore_signal(
            barrier, inc=1, device_id=(lax.rem(z + d, planes) * heads + p, col), device_id_type=MESH
        )
    for d in range(1, spread):
        pl.semaphore_signal(barrier, inc=1, device_id=(seq, lax.rem(col + d, spread)), device_id_type=MESH)

    def lanes(h):
        return pl.ds(pl.multiple_of(h * HD, HD), HD)

    def chunk(r):
        return pl.ds(r * rows, rows)

    def start_of(block):
        return sg_ref[block]

    def flag(condition):
        return jnp.where(condition, 1.0, 0.0).astype(f32)

    def plane_copy(phase, src, dst, at_src, at_dst, r, peer):
        return pltpu.make_async_remote_copy(
            src_ref=src.at[at_src, chunk(r)],
            dst_ref=dst.at[at_dst, chunk(r)],
            send_sem=plane_send.at[phase, r, peer],
            recv_sem=plane_recv.at[phase, r, at_dst],
            device_id=(base + peer, col),
            device_id_type=MESH,
        )

    def plane_start(phase, src, dst, r, peer):
        plane_copy(phase, src, dst, peer, p, r, peer).start()

    def plane_wait(phase, src, dst, r, peer):
        copy = plane_copy(phase, src, dst, peer, peer, r, peer)
        copy.wait_send()
        copy.wait_recv()

    def z_copy(phase, src, dst, r, at_dst, peer):
        return pltpu.make_async_remote_copy(
            src_ref=src.at[chunk(r)],
            dst_ref=dst.at[at_dst, chunk(r)],
            send_sem=z_send.at[phase, r, peer],
            recv_sem=z_recv.at[phase, r, at_dst],
            device_id=(peer * heads + p, col),
            device_id_type=MESH,
        )

    doc_row = jnp.broadcast_to(doc_ref[...].astype(f32), (tokens, tokens))
    doc_col = doc_row.T
    causal = lax.broadcasted_iota(jnp.int32, (tokens, tokens), 0) >= lax.broadcasted_iota(
        jnp.int32, (tokens, tokens), 1
    )
    same_ref[...] = jnp.where(causal & (doc_row == doc_col), 1.0, 0.0)
    mine = doc_col[:, :HD]
    first_ref[...] = jnp.where(mine == mine[:1], 1.0, 0.0).astype(bf16)
    last_ref[...] = jnp.where(mine == mine[tokens - 1 :], 1.0, 0.0).astype(bf16)

    for d in range(1, heads + 1):
        h = plane_peer(d)
        tail = dot(k_ref[:, lanes(h)] * last_ref[...], v_ref[:, lanes(h)], TN).astype(bf16)
        if d < heads:
            tail_out[h] = tail
        else:
            tail_in[p] = tail
    pl.semaphore_wait(barrier, heads + planes + spread - 3)
    for r in range(CHUNKS):
        for d in range(1, heads):
            plane_start(0, tail_out, tail_in, r, plane_peer(d))

    def local_forward(h, _):
        scores = dot(q_ref[:, lanes(h)], k_ref[:, lanes(h)], NT)
        weights = jnp.where(same_ref[...] > 0.5, scores, 0.0).astype(bf16)
        weights_ref[h] = weights
        att_ref[:, lanes(h)] = dot(weights, v_ref[:, lanes(h)], NN)
        return _

    lax.fori_loop(0, heads // 2, local_forward, 0)

    groups = planes * heads
    after = jnp.minimum(base + heads, groups - 1)
    for r in range(CHUNKS):
        for d in range(1, heads):
            plane_wait(0, tail_out, tail_in, r, plane_peer(d))
        run = jnp.zeros((rows, HD), f32)
        pre_ref[0, chunk(r)] = run
        for i in range(1, heads + 1):
            begin = start_of(base + i) if i < heads else start_of(after)
            joined = flag(begin < base + i - 1) * run + tail_in[i - 1, chunk(r)].astype(f32)
            run = flag(begin <= base + i - 1) * joined
            if i < heads:
                pre_ref[i, chunk(r)] = run
        agg_out[chunk(r)] = run.astype(bf16)

        def send_up(to, _, r=r):
            z_copy(0, agg_out, agg_in, r, z, to).start()
            return _

        lax.fori_loop(z + 1, planes, send_up, 0)

    lax.fori_loop(heads // 2, heads, local_forward, 0)

    begin_plane = start_of(base)
    for r in range(CHUNKS):

        def join(at, total, r=r):
            z_copy(0, agg_out, agg_in, r, at, at).wait_recv()
            return total + flag(begin_plane <= at * heads + heads - 1) * agg_in[at, chunk(r)].astype(f32)

        total = lax.fori_loop(0, z, join, jnp.zeros((rows, HD), f32))
        for d in range(1, heads + 1):
            i = plane_peer(d)
            carry = (pre_ref[i, chunk(r)] + flag(start_of(base + i) < base) * total).astype(bf16)
            if d < heads:
                carry_out[i, chunk(r)] = carry
                plane_start(1, carry_out, carry_in, r, i)
            else:
                carry_in[p, chunk(r)] = carry

    square = jnp.zeros((tokens, HD), f32)
    cross = jnp.zeros((tokens, HD), f32)
    for d in range(heads):
        h = plane_peer(d)
        if d > 0:
            for r in range(CHUNKS):
                plane_wait(1, carry_out, carry_in, r, h)
        att = att_ref[:, lanes(h)] + dot(q_ref[:, lanes(h)] * first_ref[...], carry_in[h], NN)
        att_ref[:, lanes(h)] = att
        square = square + att * att
        cross = cross + gain_ref[:, lanes(h)] * g_ref[:, lanes(h)].astype(f32) * att
    sums_out[0:1] = jnp.sum(square.T, axis=0, keepdims=True)
    sums_out[1:2] = jnp.sum(cross.T, axis=0, keepdims=True)

    def x_copy(at_dst, peer):
        return pltpu.make_async_remote_copy(
            src_ref=sums_out,
            dst_ref=sums_in.at[at_dst],
            send_sem=x_send.at[peer],
            recv_sem=x_recv.at[at_dst],
            device_id=(seq, peer),
            device_id_type=MESH,
        )

    for d in range(1, spread):
        x_copy(col, lax.rem(col + d, spread)).start()
    sums = sums_out[...]
    for d in range(1, spread):
        peer = lax.rem(col + d, spread)
        copy = x_copy(peer, peer)
        copy.wait_send()
        copy.wait_recv()
        sums = sums + sums_in[peer]
    inverse = lax.rsqrt(sums[0:1] / width + EPSILON)
    coef = inverse * inverse * inverse * sums[1:2] / width
    inv_ref[...] = jnp.broadcast_to(inverse, (HD, tokens)).T
    coef_ref[...] = jnp.broadcast_to(coef, (HD, tokens)).T

    for d in range(1, heads + 1):
        h = plane_peer(d)
        scaled = inv_ref[...] * gain_ref[:, lanes(h)]
        ga = (scaled * g_ref[:, lanes(h)].astype(f32) - coef_ref[...] * att_ref[:, lanes(h)]).astype(bf16)
        ga_ref[:, lanes(h)] = ga
        state = dot(q_ref[:, lanes(h)] * first_ref[...], ga, TN).astype(bf16)
        if d < heads:
            head_out[h] = state
            for r in range(CHUNKS):
                plane_start(2, head_out, head_in, r, h)
        else:
            head_in[p] = state

    def local_backward(h, _):
        ga = ga_ref[:, lanes(h)]
        normed_ref[:, lanes(h)] = (att_ref[:, lanes(h)] * inv_ref[...] * gain_ref[:, lanes(h)]).astype(bf16)
        scores = dot(ga, v_ref[:, lanes(h)], NT)
        scores = jnp.where(same_ref[...] > 0.5, scores, 0.0).astype(bf16)
        part = dot(ga * first_ref[...], carry_in[h], NT)
        gq_ref[:, lanes(h)] = (dot(scores, k_ref[:, lanes(h)], NN) + part).astype(bf16)
        gk_acc[:, lanes(h)] = dot(scores, q_ref[:, lanes(h)], TN)
        gv_acc[:, lanes(h)] = dot(weights_ref[h], ga, TN)
        return _

    lax.fori_loop(0, heads // 2, local_backward, 0)

    for r in range(CHUNKS):
        for d in range(1, heads):
            plane_wait(2, head_out, head_in, r, plane_peer(d))
        total = jnp.zeros((rows, HD), f32)
        for i in range(heads):
            total = total + flag(start_of(base + i) < base) * head_in[i, chunk(r)].astype(f32)
        bagg_out[chunk(r)] = total.astype(bf16)

        def send_down(to, _, r=r):
            z_copy(1, bagg_out, bagg_in, r, z, to).start()
            return _

        lax.fori_loop(0, z, send_down, 0)
        run = jnp.zeros((rows, HD), f32)
        suf_ref[heads - 1, chunk(r)] = run
        for i in range(heads - 2, -1, -1):
            begin = start_of(base + i + 1)
            if i + 2 < heads:
                run = flag(start_of(base + i + 2) <= base + i) * run
            run = flag(begin <= base + i) * (run + head_in[i + 1, chunk(r)].astype(f32))
            suf_ref[i, chunk(r)] = run

    lax.fori_loop(heads // 2, heads, local_backward, 0)

    open_after = jnp.where(z < planes - 1, start_of(after), groups)
    for r in range(CHUNKS):

        def join_back(at, total, r=r):
            z_copy(1, bagg_out, bagg_in, r, at, at).wait_recv()
            return total + flag(start_of(at * heads) <= base + heads - 1) * bagg_in[at, chunk(r)].astype(f32)

        total = lax.fori_loop(z + 1, planes, join_back, jnp.zeros((rows, HD), f32))
        for d in range(1, heads + 1):
            i = plane_peer(d)
            state = (suf_ref[i, chunk(r)] + flag(open_after <= base + i) * total).astype(bf16)
            if d < heads:
                back_out[i, chunk(r)] = state
                plane_start(3, back_out, back_in, r, i)
            else:
                back_in[p, chunk(r)] = state

    for d in range(heads):
        h = plane_peer(d)
        if d > 0:
            for r in range(CHUNKS):
                plane_wait(3, back_out, back_in, r, h)
        last = last_ref[...]
        gk_ref[:, lanes(h)] = (gk_acc[:, lanes(h)] + dot(v_ref[:, lanes(h)] * last, back_in[h], NT)).astype(bf16)
        gv_ref[:, lanes(h)] = (gv_acc[:, lanes(h)] + dot(k_ref[:, lanes(h)] * last, back_in[h], NN)).astype(bf16)

    for r in range(CHUNKS):

        def sent_up(to, _, r=r):
            z_copy(0, agg_out, agg_in, r, to, to).wait_send()
            return _

        def sent_down(to, _, r=r):
            z_copy(1, bagg_out, bagg_in, r, to, to).wait_send()
            return _

        lax.fori_loop(z + 1, planes, sent_up, 0)
        lax.fori_loop(0, z, sent_down, 0)


def solution(mesh):
    groups, spread = mesh.shape["seq"], mesh.shape["head"]

    def local(query_in, key_in, value_in, out_grad, norm_gain, doc_ids, start_group):
        tokens, columns = query_in.shape
        heads = columns // HD
        planes = groups // heads
        vmem = pl.BlockSpec(memory_space=pltpu.VMEM)
        state = pltpu.VMEM((heads, HD, HD), bf16)
        state_f = pltpu.VMEM((heads, HD, HD), f32)
        one = pltpu.VMEM((HD, HD), bf16)
        many = pltpu.VMEM((planes, HD, HD), bf16)
        row = pltpu.VMEM((tokens, HD), f32)
        scan = [state, state, state_f, one, many, state, state]
        return pl.pallas_call(
            functools.partial(kernel, planes, heads, spread, columns * spread),
            out_shape=[jax.ShapeDtypeStruct((tokens, columns), bf16)] * 4,
            in_specs=[pl.BlockSpec(memory_space=pltpu.SMEM)] + [vmem] * 6,
            out_specs=[vmem] * 4,
            scratch_shapes=[
                pltpu.VMEM((tokens, tokens), f32),
                pltpu.VMEM((tokens, HD), bf16),
                pltpu.VMEM((tokens, HD), bf16),
                row,
                row,
                pltpu.VMEM((heads, tokens, tokens), bf16),
                pltpu.VMEM((tokens, columns), f32),
                pltpu.VMEM((tokens, columns), bf16),
                pltpu.VMEM((tokens, columns), f32),
                pltpu.VMEM((tokens, columns), f32),
                *scan,
                *scan,
                pltpu.VMEM((2, tokens), f32),
                pltpu.VMEM((spread, 2, tokens), f32),
                pltpu.SemaphoreType.DMA((4, CHUNKS, heads)),
                pltpu.SemaphoreType.DMA((4, CHUNKS, heads)),
                pltpu.SemaphoreType.DMA((2, CHUNKS, planes)),
                pltpu.SemaphoreType.DMA((2, CHUNKS, planes)),
                pltpu.SemaphoreType.DMA((spread,)),
                pltpu.SemaphoreType.DMA((spread,)),
            ],
            compiler_params=pltpu.CompilerParams(collective_id=0, has_side_effects=True),
            name="attention",
        )(
            start_group,
            doc_ids.reshape(1, tokens),
            query_in,
            key_in,
            value_in,
            out_grad,
            norm_gain.reshape(1, columns),
        )

    wide = P("seq", "head")
    return jax.shard_map(
        local,
        mesh=mesh,
        in_specs=(wide, wide, wide, wide, P("head"), P("seq"), P()),
        out_specs=(wide, wide, wide, wide),
        check_vma=False,
    )
```

time: 660 us -> 60.5 us (0.09); the launches traced: 652 us -> 60.3 us
  other arithmetic: 171 us -> 0 us
  blocking collectives: 141 us -> 0 us
  waiting for transfers between devices: 135 us -> 0 us
  loops' own time: 87.1 us -> 0 us
  local copies, waits for them, and re-layouts: 88.8 us -> 5.18 us
  Pallas kernels: 0 us -> 54.4 us
  between operations: 17 us -> 0.65 us
  matrix products: 12.4 us -> 0 us
    select_n x128 -> x0, other arithmetic: 167 us -> none  [lap(): return jax.tree.map(lambda a, b: jnp.where(reached, a, b), new, before)]
    all_gather x2 -> x0, waiting for transfers between devices: 135 us -> none  [prefix(): everything = jax.tree.map(lambda part: lax.all_gather(part, axis), x)]
    unnamed x1 -> x0, blocking collectives: 132 us -> none
    another operation x2 -> x0, loops' own time: 87.1 us -> none  [prefix(): return lax.fori_loop(0, length, lap, start)]
    dynamic_slice x129 -> x0, local copies, waits for them, and re-layouts: 75.9 us -> none  [the longest x128 75.2 us: lap(): new = combine(before, jax.tree.map(lambda part: part[at], everything))]
    pallas_call x0 -> x1, Pallas kernels: none -> 54.4 us  [local(): pl.pallas_call(functools.partial(kernel, planes, heads, spread, columns *...]
    dot_general x12 -> x0, matrix products: 12.4 us -> none  [the longest x1 2.7 us: local(): jnp.einsum('tha,hab->thb', query_h, carry_b, preferred_element_type=jnp.f...]
    psum x1 -> x0, blocking collectives: 8.36 us -> none  [local(): square_total = lax.psum(square_part, 'head')]
  transfers between devices with their start and end apart: 2 -> 0, of which waited for: 2 -> 0; matrix products, arithmetic and copies ran while one was open for 2% -> 0% of each run, Pallas kernels for 0% -> 0%
where the time goes in v1:
time: 60.5 us; the launch traced here: 60.3 us
  Pallas kernels  54.4 us (90%)
  local copies, waits for them, and re-layouts  5.18 us (9%)
  between operations  0.65 us (1%)
    pallas_call x1, Pallas kernels, local(): pl.pallas_call(functools.partial(kernel, planes, heads, spread, columns *...  54.4 us
    unnamed x10, local copies, waits for them, and re-layouts  5.18 us

profile of v1, /device:TPU:1, one launch (start us, length us, event | category | flops | bytes accessed | tf_op | source)
XLA Modules:
  0.0 60.3 jit_solution(6163033699452238686)
XLA Ops:
  0.6 54.4 %attention.1 = (bf16[256,1024]{1,0:T(8,128)(2,1)}, bf16[256,1024]{1,0:T(8,128)(2,1)}, bf16[256,1024]{1,0:T(8,128)(2,1)}, bf16[256,1024]{1,0:T(8,128)(2,1)}) custom-call(s32[64]{0:T(128)} %sg_ref.1, s32[1,256]{1,0:T(1,128)} %bitcast.3, bf16[256,1024]{1,0:T(8,128)(2,1)} %q_ref.1, bf16[256,1024]{1,0:T(8,128)(2,1)} %k_ref.1, bf16[256,1024]{1,0:T(8,128)(2,1)} %v_ref.1, ...), custom_call_target="tpu_custom_call" | custom-call | tf_op jit(solution)/shard_map/attention/pallas_call | solution.py:309
  55.1 0.0 copy-start.2
  55.1 1.9 %copy.15 = bf16[256,1024]{1,0:T(8,128)(2,1)} copy(bf16[256,1024]{1,0:T(8,128)(2,1)} %get-tuple-element.8) | data formatting | bytes 1048576
  57.0 0.0 copy-done.2
  57.0 0.0 copy-start.1
  57.0 0.8 %copy.16 = bf16[256,1024]{1,0:T(8,128)(2,1)} copy(bf16[256,1024]{1,0:T(8,128)(2,1)S(1)} %copy-done.2) | data formatting | bytes 1048576
  57.8 0.4 copy-done.1
  58.2 0.0 copy-start
  58.2 0.8 %copy.17 = bf16[256,1024]{1,0:T(8,128)(2,1)} copy(bf16[256,1024]{1,0:T(8,128)(2,1)S(1)} %copy-done.1) | data formatting | bytes 1048576
  59.0 0.4 copy-done
  59.5 0.8 %copy.18 = bf16[256,1024]{1,0:T(8,128)(2,1)} copy(bf16[256,1024]{1,0:T(8,128)(2,1)S(1)} %copy-done) | data formatting | bytes 1048576
Async XLA Ops:
  55.1 1.9 %copy-start.2 = (bf16[256,1024]{1,0:T(8,128)(2,1)S(1)}, bf16[256,1024]{1,0:T(8,128)(2,1)}, u32[]{:S(2)}) copy-start(bf16[256,1024]{1,0:T(8,128)(2,1)} %get-tuple-element.9) | copy-start | bytes 1572868
  57.0 1.2 %copy-start.1 = (bf16[256,1024]{1,0:T(8,128)(2,1)S(1)}, bf16[256,1024]{1,0:T(8,128)(2,1)}, u32[]{:S(2)}) copy-start(bf16[256,1024]{1,0:T(8,128)(2,1)} %get-tuple-element.10) | copy-start | bytes 1572868
  58.2 1.2 %copy-start = (bf16[256,1024]{1,0:T(8,128)(2,1)S(1)}, bf16[256,1024]{1,0:T(8,128)(2,1)}, u32[]{:S(2)}) copy-start(bf16[256,1024]{1,0:T(8,128)(2,1)} %get-tuple-element.11) | copy-start | bytes 1572868

commit v2 on v1

--- a/solution.py
+++ b/solution.py
@@ -292,6 +292,17 @@
         lax.fori_loop(0, z, sent_down, 0)
 
 
+def write(a, b, c, d, a_out, b_out, c_out, d_out, sem):
+    copies = [
+        pltpu.make_async_copy(src, dst, sem.at[i])
+        for i, (src, dst) in enumerate(((a, a_out), (b, b_out), (c, c_out), (d, d_out)))
+    ]
+    for copy in copies:
+        copy.start()
+    for copy in copies:
+        copy.wait()
+
+
 def solution(mesh):
     groups, spread = mesh.shape["seq"], mesh.shape["head"]
 
@@ -306,9 +317,9 @@
         many = pltpu.VMEM((planes, HD, HD), bf16)
         row = pltpu.VMEM((tokens, HD), f32)
         scan = [state, state, state_f, one, many, state, state]
-        return pl.pallas_call(
+        outs = pl.pallas_call(
             functools.partial(kernel, planes, heads, spread, columns * spread),
-            out_shape=[jax.ShapeDtypeStruct((tokens, columns), bf16)] * 4,
+            out_shape=[pltpu.VMEM((tokens, columns), bf16)] * 4,
             in_specs=[pl.BlockSpec(memory_space=pltpu.SMEM)] + [vmem] * 6,
             out_specs=[vmem] * 4,
             scratch_shapes=[
@@ -344,6 +355,15 @@
             out_grad,
             norm_gain.reshape(1, columns),
         )
+        return pl.pallas_call(
+            write,
+            out_shape=[jax.ShapeDtypeStruct((tokens, columns), bf16)] * 4,
+            in_specs=[vmem] * 4,
+            out_specs=[pl.BlockSpec(memory_space=pl.ANY)] * 4,
+            scratch_shapes=[pltpu.SemaphoreType.DMA((4,))],
+            compiler_params=pltpu.CompilerParams(vmem_limit_bytes=1 << 20),
+            name="write",
+        )(*outs)
 
     wide = P("seq", "head")
     return jax.shard_map(

time: 60.5 us -> 55.2 us (0.912)
  local copies, waits for them, and re-layouts: 5.18 us -> 0 us
    unnamed x10 -> x0, local copies, waits for them, and re-layouts: 5.18 us -> none
    pallas_call x0 -> x1, Pallas kernels: none -> 1.35 us  [local(): pl.pallas_call(write, out_shape=[jax.ShapeDtypeStruct((tokens, columns),...]
    pallas_call x1, Pallas kernels: 54.4 us -> 53.1 us  [local(): pl.pallas_call(functools.partial(kernel, planes, heads, spread, columns *...]
where the time goes in v2:
time: 55.2 us; the launch traced here: 55.1 us
  Pallas kernels  54.4 us (99%)
  between operations  0.64 us (1%)
    pallas_call x1, Pallas kernels, local(): pl.pallas_call(functools.partial(kernel, planes, heads, spread, columns *...  53.1 us
    pallas_call x1, Pallas kernels, local(): pl.pallas_call(write, out_shape=[jax.ShapeDtypeStruct((tokens, columns),...  1.35 us

profile of v2, /device:TPU:1, one launch (start us, length us, event | category | flops | bytes accessed | tf_op | source)
XLA Modules:
  0.0 55.1 jit_solution(17446373826980556222)
XLA Ops:
  0.6 53.1 %attention.1 = (bf16[256,1024]{1,0:T(8,128)(2,1)S(1)}, bf16[256,1024]{1,0:T(8,128)(2,1)S(1)}, bf16[256,1024]{1,0:T(8,128)(2,1)S(1)}, bf16[256,1024]{1,0:T(8,128)(2,1)S(1)}) custom-call(s32[64]{0:T(128)} %sg_ref.1, s32[1,256]{1,0:T(1,128)} %bitcast.3, bf16[256,1024]{1,0:T(8,128)(2,1)} %q_ref.1, bf16[256,1024]{1,0:T(8,128)(2,1)} %k_ref.1, ...), custom_call_target="tpu_custom_call" | custom-call | tf_op jit(solution)/shard_map/attention/pallas_call | solution.py:320
  53.7 1.3 %write.1 = (bf16[256,1024]{1,0:T(8,128)(2,1)}, bf16[256,1024]{1,0:T(8,128)(2,1)}, bf16[256,1024]{1,0:T(8,128)(2,1)}, bf16[256,1024]{1,0:T(8,128)(2,1)}) custom-call(bf16[256,1024]{1,0:T(8,128)(2,1)S(1)} %get-tuple-element.8.a, bf16[256,1024]{1,0:T(8,128)(2,1)S(1)} %get-tuple-element.9.b, bf16[256,1024]{1,0:T(8,128)(2,1)S(1)} %get-tuple-element.10.c, ...), custom_call_target="tpu_custom_call" | custom-call | tf_op jit(solution)/shard_map/write/pallas_call | solution.py:358

commit v3 on v2

v3 whole, which is shorter than its diff:
```python
import functools

import jax
import jax.numpy as jnp
from jax import lax
from jax.experimental import pallas as pl
from jax.experimental.pallas import tpu as pltpu
from jax.sharding import PartitionSpec as P

HD = 128
EPSILON = 1e-06
MESH = pl.DeviceIdType.MESH
f32, bf16 = jnp.float32, jnp.bfloat16


def dot(a, b, contract):
    return lax.dot_general(a, b, (contract, ((), ())), preferred_element_type=f32)


NN = ((1,), (0,))
NT = ((1,), (1,))
TN = ((0,), (0,))


def kernel(
    chips, ring, heads, spread, width,
    sg_ref, doc_ref, q_hbm, k_hbm, v_hbm, g_hbm, gain_ref,
    normed_ref, gq_ref, gk_ref, gv_ref,
    q_ref, k_ref, v_ref, g_ref,
    same_ref, first_ref, last_ref, inv_ref, coef_ref,
    weights_ref, att_ref, ga_ref, qf_ref, scaled_ref, gk_acc, gv_acc,
    pair_out, pair, sum_out, sum_in, run_out, run_in, share_out, carry_in,
    bpair_out, bpair, bsum_out, bsum_in, brun_out, brun_in, bshare_out, back_in,
    rows_out, rows_in,
    load_sem, chip_send, chip_recv, core_send, core_recv, x_send, x_recv,
):
    seq, col = lax.axis_index("seq"), lax.axis_index("head")
    chip, core = lax.div(seq, 2), lax.rem(seq, 2)
    partner = seq + 1 - 2 * core
    tokens = q_ref.shape[0]
    half = heads // 2
    piece = sum_out.shape[1]
    pieces = HD // piece
    mine, theirs = core * half, (1 - core) * half
    c0, c1, groups = 2 * chip, 2 * chip + 1, 2 * chips
    c2 = jnp.minimum(c0 + 2, groups - 1)
    lines = chips // ring

    loads = [
        pltpu.make_async_copy(src, dst, load_sem.at[i])
        for i, (src, dst) in enumerate(((k_hbm, k_ref), (v_hbm, v_ref), (q_hbm, q_ref), (g_hbm, g_ref)))
    ]
    for load in loads:
        load.start()

    def hops(offset, size):
        return min(offset, size - offset)

    offsets = sorted(
        ((dz, dy) for dz in range(lines) for dy in range(ring) if dz or dy),
        key=lambda o: -(hops(o[0], lines) + hops(o[1], ring)),
    )
    chip_z, chip_y = lax.div(chip, ring), lax.rem(chip, ring)
    others = [lax.rem(chip_z + dz, lines) * ring + lax.rem(chip_y + dy, ring) for dz, dy in offsets]

    barrier = pltpu.get_barrier_semaphore()
    for other in others:
        pl.semaphore_signal(barrier, inc=1, device_id=(2 * other + core, col), device_id_type=MESH)
    for d in range(1, spread):
        pl.semaphore_signal(barrier, inc=1, device_id=(seq, lax.rem(col + d, spread)), device_id_type=MESH)
    pl.semaphore_signal(barrier, inc=1, device_id=(partner, col), device_id_type=MESH)

    def lanes(h):
        return pl.ds(pl.multiple_of(h * HD, HD), HD)

    def flag(condition):
        return jnp.where(condition, 1.0, 0.0).astype(f32)

    def core_copy(phase, src, dst, at_src, at_dst, slot):
        return pltpu.make_async_remote_copy(
            src_ref=src.at[at_src],
            dst_ref=dst.at[at_dst],
            send_sem=core_send.at[phase, slot],
            recv_sem=core_recv.at[phase, slot],
            device_id=(partner, col),
            device_id_type=MESH,
        )

    def chip_copy(phase, src, dst, at_src, at_dst, other):
        return pltpu.make_async_remote_copy(
            src_ref=src.at[at_src],
            dst_ref=dst.at[at_dst],
            send_sem=chip_send.at[phase, at_src],
            recv_sem=chip_recv.at[phase, at_dst],
            device_id=(2 * other + core, col),
            device_id_type=MESH,
        )

    def chip_start(phase, src, dst):
        for other in others:
            chip_copy(phase, src, dst, other, chip, other).start()

    def chip_wait(phase, src, dst):
        def one(d, carry):
            other = lax.rem(chip + d, chips)
            chip_copy(phase, src, dst, other, other, other).wait_recv()
            return carry

        lax.fori_loop(1, chips, one, 0)

    def chip_sent(phase, src, dst):
        def one(d, carry):
            other = lax.rem(chip + d, chips)
            chip_copy(phase, src, dst, other, other, other).wait_send()
            return carry

        lax.fori_loop(1, chips, one, 0)

    def put(ref, j, state):
        ref[pl.ds(j * pieces, pieces)] = state.astype(bf16).reshape(pieces, piece, HD)

    def take(ref, j):
        return ref[pl.ds(j * pieces, pieces)].reshape(HD, HD).astype(f32)

    doc_row = jnp.broadcast_to(doc_ref[...].astype(f32), (tokens, tokens))
    doc_col = doc_row.T
    causal = lax.broadcasted_iota(jnp.int32, (tokens, tokens), 0) >= lax.broadcasted_iota(
        jnp.int32, (tokens, tokens), 1
    )
    same_ref[...] = jnp.where(causal & (doc_row == doc_col), 1.0, 0.0)
    own = doc_col[:, :HD]
    first_ref[...] = jnp.where(own == own[:1], 1.0, 0.0).astype(bf16)
    last_ref[...] = jnp.where(own == own[tokens - 1 :], 1.0, 0.0).astype(bf16)

    loads[0].wait()
    loads[1].wait()
    for j in range(half):
        at = lanes(theirs + j)
        pair_out[j] = dot(k_ref[:, at] * last_ref[...], v_ref[:, at], TN)
    pl.semaphore_wait(barrier, chips + spread - 1)
    for j in range(half):
        core_copy(0, pair_out, pair.at[core], j, j, j).start()
    for j in range(half):
        at = lanes(mine + j)
        pair[core, j] = dot(k_ref[:, at] * last_ref[...], v_ref[:, at], TN)

    both = flag(sg_ref[c2] <= c0)
    for j in range(half):
        core_copy(0, pair_out, pair.at[1 - core], j, j, j).wait_recv()
        put(sum_out, j, pair[1, j] + both * pair[0, j])
    sum_in[chip] = sum_out[chip]
    chip_start(0, sum_out, sum_in)

    loads[2].wait()
    loads[3].wait()

    def local_forward(h, _):
        at = lanes(h)
        scores = dot(q_ref[:, at], k_ref[:, at], NT)
        weights = jnp.where(same_ref[...] > 0.5, scores, 0.0).astype(bf16)
        weights_ref[h] = weights
        att_ref[:, at] = dot(weights, v_ref[:, at], NN)
        qf_ref[:, at] = q_ref[:, at] * first_ref[...]
        scaled_ref[:, at] = gain_ref[:, at] * g_ref[:, at].astype(f32)
        return _

    lax.fori_loop(0, heads, local_forward, 0)

    chip_wait(0, sum_out, sum_in)
    run = jnp.zeros((piece, HD), f32)
    run_out[0] = run.astype(bf16)
    for w in range(1, chips):
        begin = sg_ref[2 * w]
        run = flag(begin <= 2 * w - 1) * (sum_in[w - 1].astype(f32) + flag(begin < 2 * w - 2) * run)
        run_out[w] = run.astype(bf16)
    run_in[chip] = run_out[chip]
    chip_start(1, run_out, run_in)
    chip_wait(1, run_out, run_in)

    odd = core == 1
    inside, through = flag(sg_ref[c1] <= c0), flag(sg_ref[c1] < c0)
    own_a, own_b = jnp.where(odd, inside, 0.0), jnp.where(odd, through, 1.0)
    their_a, their_b = jnp.where(odd, 0.0, inside), jnp.where(odd, 1.0, through)
    for j in range(half):
        share_out[j] = (their_a * pair[0, j] + their_b * take(run_in, j)).astype(bf16)
        core_copy(1, share_out, carry_in, j, mine + j, j).start()
    for j in range(half):
        carry_in[mine + j] = (own_a * pair[0, j] + own_b * take(run_in, j)).astype(bf16)

    square = jnp.zeros((tokens, HD), f32)
    cross = jnp.zeros((tokens, HD), f32)
    for i in range(heads):
        j = i % half
        h = mine + j if i < half else theirs + j
        at = lanes(h)
        if i >= half:
            core_copy(1, share_out, carry_in, j, h, j).wait_recv()
        att = att_ref[:, at] + dot(qf_ref[:, at], carry_in[h], NN)
        att_ref[:, at] = att
        square = square + att * att
        cross = cross + scaled_ref[:, at] * att
    rows_out[0:1] = jnp.sum(square.T, axis=0, keepdims=True)
    rows_out[1:2] = jnp.sum(cross.T, axis=0, keepdims=True)

    def x_copy(at_dst, peer):
        return pltpu.make_async_remote_copy(
            src_ref=rows_out,
            dst_ref=rows_in.at[at_dst],
            send_sem=x_send.at[peer],
            recv_sem=x_recv.at[at_dst],
            device_id=(seq, peer),
            device_id_type=MESH,
        )

    for d in range(1, spread):
        x_copy(col, lax.rem(col + d, spread)).start()
    sums = rows_out[...]
    for d in range(1, spread):
        peer = lax.rem(col + d, spread)
        x_copy(peer, peer).wait_recv()
        sums = sums + rows_in[peer]
    inverse = lax.rsqrt(sums[0:1] / width + EPSILON)
    coef = inverse * inverse * inverse * sums[1:2] / width
    inv_ref[...] = jnp.broadcast_to(inverse, (HD, tokens)).T
    coef_ref[...] = jnp.broadcast_to(coef, (HD, tokens)).T

    for i in range(heads):
        j = i % half
        h = theirs + j if i < half else mine + j
        at = lanes(h)
        ga = (inv_ref[...] * scaled_ref[:, at] - coef_ref[...] * att_ref[:, at]).astype(bf16)
        ga_ref[:, at] = ga
        state = dot(qf_ref[:, at], ga, TN)
        if i < half:
            bpair_out[j] = state
            core_copy(2, bpair_out, bpair.at[core], j, j, j).start()
        else:
            bpair[core, j] = state

    from_first, from_second = flag(sg_ref[c0] < c0), flag(sg_ref[c1] < c0)
    for j in range(half):
        core_copy(2, bpair_out, bpair.at[1 - core], j, j, j).wait_recv()
        put(bsum_out, j, from_first * bpair[0, j] + from_second * bpair[1, j])
    bsum_in[chip] = bsum_out[chip]
    chip_start(2, bsum_out, bsum_in)

    def local_backward(h, _):
        at = lanes(h)
        ga = ga_ref[:, at]
        normed_ref[:, at] = (att_ref[:, at] * inv_ref[...] * gain_ref[:, at]).astype(bf16)
        scores = dot(ga, v_ref[:, at], NT)
        scores = jnp.where(same_ref[...] > 0.5, scores, 0.0).astype(bf16)
        part = dot(ga * first_ref[...], carry_in[h], NT)
        gq_ref[:, at] = (dot(scores, k_ref[:, at], NN) + part).astype(bf16)
        gk_acc[:, at] = dot(scores, q_ref[:, at], TN)
        gv_acc[:, at] = dot(weights_ref[h], ga, TN)
        return _

    lax.fori_loop(0, half, local_backward, 0)

    chip_wait(2, bsum_out, bsum_in)
    run = jnp.zeros((piece, HD), f32)
    brun_out[chips - 1] = run.astype(bf16)
    for w in range(chips - 2, -1, -1):
        run = flag(sg_ref[min(2 * w + 4, groups - 1)] <= 2 * w + 1) * run
        run = flag(sg_ref[2 * w + 2] <= 2 * w + 1) * (bsum_in[w + 1].astype(f32) + run)
        brun_out[w] = run.astype(bf16)
    brun_in[chip] = brun_out[chip]
    chip_start(3, brun_out, brun_in)

    lax.fori_loop(half, heads, local_backward, 0)

    chip_wait(3, brun_out, brun_in)
    reach = flag(sg_ref[c2] <= c0)
    own_a, own_b = jnp.where(odd, 0.0, inside), jnp.where(odd, 1.0, reach)
    their_a, their_b = jnp.where(odd, inside, 0.0), jnp.where(odd, reach, 1.0)
    for j in range(half):
        bshare_out[j] = (their_a * bpair[1, j] + their_b * take(brun_in, j)).astype(bf16)
        core_copy(3, bshare_out, back_in, j, mine + j, j).start()
    for j in range(half):
        back_in[mine + j] = (own_a * bpair[1, j] + own_b * take(brun_in, j)).astype(bf16)

    for i in range(heads):
        j = i % half
        h = mine + j if i < half else theirs + j
        at = lanes(h)
        if i >= half:
            core_copy(3, bshare_out, back_in, j, h, j).wait_recv()
        last = last_ref[...]
        gk_ref[:, at] = (gk_acc[:, at] + dot(v_ref[:, at] * last, back_in[h], NT)).astype(bf16)
        gv_ref[:, at] = (gv_acc[:, at] + dot(k_ref[:, at] * last, back_in[h], NN)).astype(bf16)

    for phase, src, dst in ((0, sum_out, sum_in), (1, run_out, run_in), (2, bsum_out, bsum_in), (3, brun_out, brun_in)):
        chip_sent(phase, src, dst)
    for j in range(half):
        core_copy(0, pair_out, pair.at[core], j, j, j).wait_send()
        core_copy(1, share_out, carry_in, j, mine + j, j).wait_send()
        core_copy(2, bpair_out, bpair.at[core], j, j, j).wait_send()
        core_copy(3, bshare_out, back_in, j, mine + j, j).wait_send()
    for d in range(1, spread):
        peer = lax.rem(col + d, spread)
        x_copy(col, peer).wait_send()


def write(a, b, c, d, a_out, b_out, c_out, d_out, sem):
    copies = [
        pltpu.make_async_copy(src, dst, sem.at[i])
        for i, (src, dst) in enumerate(((a, a_out), (b, b_out), (c, c_out), (d, d_out)))
    ]
    for copy in copies:
        copy.start()
    for copy in copies:
        copy.wait()


def solution(mesh):
    groups, spread = mesh.shape["seq"], mesh.shape["head"]
    chips = groups // 2
    ring = 4 if chips % 4 == 0 else 1

    def local(query_in, key_in, value_in, out_grad, norm_gain, doc_ids, start_group):
        tokens, columns = query_in.shape
        heads = columns // HD
        half = heads // 2
        vmem = pl.BlockSpec(memory_space=pltpu.VMEM)
        hbm = pl.BlockSpec(memory_space=pltpu.HBM)
        states = pltpu.VMEM((half, HD, HD), f32)
        pair = pltpu.VMEM((2, half, HD, HD), f32)
        pieces = pltpu.VMEM((chips, half * HD // chips, HD), bf16)
        narrow = pltpu.VMEM((tokens, HD), bf16)
        row = pltpu.VMEM((tokens, HD), f32)
        wide_b = pltpu.VMEM((tokens, columns), bf16)
        wide_f = pltpu.VMEM((tokens, columns), f32)
        scan = [states, pair, pieces, pieces, pieces, pieces]
        scan += [pltpu.VMEM((half, HD, HD), bf16), pltpu.VMEM((heads, HD, HD), bf16)]
        outs = pl.pallas_call(
            functools.partial(kernel, chips, ring, heads, spread, columns * spread),
            out_shape=[pltpu.VMEM((tokens, columns), bf16)] * 4,
            in_specs=[pl.BlockSpec(memory_space=pltpu.SMEM), vmem] + [hbm] * 4 + [vmem],
            out_specs=[vmem] * 4,
            scratch_shapes=[
                *[wide_b] * 4,
                pltpu.VMEM((tokens, tokens), f32),
                narrow,
                narrow,
                row,
                row,
                pltpu.VMEM((heads, tokens, tokens), bf16),
                wide_f,
                wide_b,
                wide_b,
                wide_f,
                wide_f,
                wide_f,
                *scan,
                *scan,
                pltpu.VMEM((2, tokens), f32),
                pltpu.VMEM((spread, 2, tokens), f32),
                pltpu.SemaphoreType.DMA((4,)),
                pltpu.SemaphoreType.DMA((4, chips)),
                pltpu.SemaphoreType.DMA((4, chips)),
                pltpu.SemaphoreType.DMA((4, half)),
                pltpu.SemaphoreType.DMA((4, half)),
                pltpu.SemaphoreType.DMA((spread,)),
                pltpu.SemaphoreType.DMA((spread,)),
            ],
            compiler_params=pltpu.CompilerParams(collective_id=0, has_side_effects=True),
            name="attention",
        )(
            start_group,
            doc_ids.reshape(1, tokens),
            query_in,
            key_in,
            value_in,
            out_grad,
            norm_gain.reshape(1, columns),
        )
        return pl.pallas_call(
            write,
            out_shape=[jax.ShapeDtypeStruct((tokens, columns), bf16)] * 4,
            in_specs=[vmem] * 4,
            out_specs=[pl.BlockSpec(memory_space=pl.ANY)] * 4,
            scratch_shapes=[pltpu.SemaphoreType.DMA((4,))],
            compiler_params=pltpu.CompilerParams(vmem_limit_bytes=1 << 20),
            name="write",
        )(*outs)

    wide = P("seq", "head")
    return jax.shard_map(
        local,
        mesh=mesh,
        in_specs=(wide, wide, wide, wide, P("head"), P("seq"), P()),
        out_specs=(wide, wide, wide, wide),
        check_vma=False,
    )
```

time: 55.2 us -> 55.1 us (level)
  no operation moved by 1% of the time
where the time goes in v3:
time: 55.1 us; the launch traced here: 54.9 us
  Pallas kernels  54.3 us (99%)
  between operations  0.64 us (1%)
    pallas_call x1, Pallas kernels, local(): pl.pallas_call(functools.partial(kernel, chips, ring, heads, spread, colu...  52.9 us
    pallas_call x1, Pallas kernels, local(): pl.pallas_call(write, out_shape=[jax.ShapeDtypeStruct((tokens, columns),...  1.35 us

profile of v3, /device:TPU:1, one launch (start us, length us, event | category | flops | bytes accessed | tf_op | source)
XLA Modules:
  0.0 54.9 jit_solution(1641003818419496544)
XLA Ops:
  0.6 52.9 %attention.1 = (bf16[256,1024]{1,0:T(8,128)(2,1)S(1)}, bf16[256,1024]{1,0:T(8,128)(2,1)S(1)}, bf16[256,1024]{1,0:T(8,128)(2,1)S(1)}, bf16[256,1024]{1,0:T(8,128)(2,1)S(1)}) custom-call(s32[64]{0:T(128)} %sg_ref.1, s32[1,256]{1,0:T(1,128)} %bitcast.3, bf16[256,1024]{1,0:T(8,128)(2,1)} %q_hbm.1, bf16[256,1024]{1,0:T(8,128)(2,1)} %k_hbm.1, ...), custom_call_target="tpu_custom_call" | custom-call | tf_op jit(solution)/shard_map/attention/pallas_call | solution.py:336
  53.6 1.3 %write.1 = (bf16[256,1024]{1,0:T(8,128)(2,1)}, bf16[256,1024]{1,0:T(8,128)(2,1)}, bf16[256,1024]{1,0:T(8,128)(2,1)}, bf16[256,1024]{1,0:T(8,128)(2,1)}) custom-call(bf16[256,1024]{1,0:T(8,128)(2,1)S(1)} %get-tuple-element.8.a, bf16[256,1024]{1,0:T(8,128)(2,1)S(1)} %get-tuple-element.9.b, bf16[256,1024]{1,0:T(8,128)(2,1)S(1)} %get-tuple-element.10.c, ...), custom_call_target="tpu_custom_call" | custom-call | tf_op jit(solution)/shard_map/write/pallas_call | solution.py:378

commit v4 on v3

--- a/solution.py
+++ b/solution.py
@@ -25,14 +25,14 @@
 def kernel(
     chips, ring, heads, spread, width,
     sg_ref, doc_ref, q_hbm, k_hbm, v_hbm, g_hbm, gain_ref,
-    normed_ref, gq_ref, gk_ref, gv_ref,
+    normed_ref, gq_ref, gk_acc, gv_acc, kl_ref, vl_ref, back_in,
     q_ref, k_ref, v_ref, g_ref,
     same_ref, first_ref, last_ref, inv_ref, coef_ref,
-    weights_ref, att_ref, ga_ref, qf_ref, scaled_ref, gk_acc, gv_acc,
+    weights_ref, att_ref, ga_ref, qf_ref, qt_ref, scaled_ref,
     pair_out, pair, sum_out, sum_in, run_out, run_in, share_out, carry_in,
-    bpair_out, bpair, bsum_out, bsum_in, brun_out, brun_in, bshare_out, back_in,
+    bpair_out, bpair, bsum_out, bsum_in, brun_out, brun_in, bshare_out,
     rows_out, rows_in,
-    load_sem, chip_send, chip_recv, core_send, core_recv, x_send, x_recv,
+    load_sem, chip_send, chip_recv, core_send, core_recv, x_send, x_recv, here, go,
 ):
     seq, col = lax.axis_index("seq"), lax.axis_index("head")
     chip, core = lax.div(seq, 2), lax.rem(seq, 2)
@@ -64,11 +64,15 @@
     others = [lax.rem(chip_z + dz, lines) * ring + lax.rem(chip_y + dy, ring) for dz, dy in offsets]
 
     barrier = pltpu.get_barrier_semaphore()
+
+    @pl.when(core == 0)
+    def _():
+        pl.semaphore_signal(barrier, inc=1, device_id=(partner, col), device_id_type=MESH)
+
     for other in others:
-        pl.semaphore_signal(barrier, inc=1, device_id=(2 * other + core, col), device_id_type=MESH)
+        pl.semaphore_signal(barrier, inc=1, device_id=(2 * other, col), device_id_type=MESH)
     for d in range(1, spread):
-        pl.semaphore_signal(barrier, inc=1, device_id=(seq, lax.rem(col + d, spread)), device_id_type=MESH)
-    pl.semaphore_signal(barrier, inc=1, device_id=(partner, col), device_id_type=MESH)
+        pl.semaphore_signal(barrier, inc=1, device_id=(c0, lax.rem(col + d, spread)), device_id_type=MESH)
 
     def lanes(h):
         return pl.ds(pl.multiple_of(h * HD, HD), HD)
@@ -90,8 +94,8 @@
         return pltpu.make_async_remote_copy(
             src_ref=src.at[at_src],
             dst_ref=dst.at[at_dst],
-            send_sem=chip_send.at[phase, at_src],
-            recv_sem=chip_recv.at[phase, at_dst],
+            send_sem=chip_send.at[phase],
+            recv_sem=chip_recv.at[phase],
             device_id=(2 * other + core, col),
             device_id_type=MESH,
         )
@@ -100,21 +104,13 @@
         for other in others:
             chip_copy(phase, src, dst, other, chip, other).start()
 
+    every = pl.ds(0, chips - 1)
+
     def chip_wait(phase, src, dst):
-        def one(d, carry):
-            other = lax.rem(chip + d, chips)
-            chip_copy(phase, src, dst, other, other, other).wait_recv()
-            return carry
-
-        lax.fori_loop(1, chips, one, 0)
+        chip_copy(phase, src, dst, every, every, others[0]).wait_recv()
 
     def chip_sent(phase, src, dst):
-        def one(d, carry):
-            other = lax.rem(chip + d, chips)
-            chip_copy(phase, src, dst, other, other, other).wait_send()
-            return carry
-
-        lax.fori_loop(1, chips, one, 0)
+        chip_copy(phase, src, dst, every, every, others[0]).wait_send()
 
     def put(ref, j, state):
         ref[pl.ds(j * pieces, pieces)] = state.astype(bf16).reshape(pieces, piece, HD)
@@ -122,7 +118,51 @@
     def take(ref, j):
         return ref[pl.ds(j * pieces, pieces)].reshape(HD, HD).astype(f32)
 
-    doc_row = jnp.broadcast_to(doc_ref[...].astype(f32), (tokens, tokens))
+    docs = doc_ref[...].astype(f32)
+    last_row = jnp.where(docs == docs[:, tokens - 1 :], 1.0, 0.0).astype(bf16)
+    first_row = jnp.where(docs == docs[:, :1], 1.0, 0.0).astype(bf16)
+
+    def tail(h):
+        at = lanes(h)
+        return dot(k_ref[:, at].T * last_row, v_ref[:, at], NN)
+
+    loads[0].wait()
+    loads[1].wait()
+    for j in range(half):
+        pair_out[j] = tail(theirs + j)
+
+    @pl.when(core == 1)
+    def _():
+        pl.semaphore_wait(barrier, 1)
+        pl.semaphore_signal(here, inc=1, device_id=(partner, col), device_id_type=MESH)
+
+    @pl.when(core == 0)
+    def _():
+        pl.semaphore_wait(here, 1)
+
+    for j in range(half):
+        core_copy(0, pair_out, pair.at[core], j, j, j).start()
+    for j in range(half):
+        pair[core, j] = tail(mine + j)
+
+    both = flag(sg_ref[c2] <= c0)
+    for j in range(half):
+        core_copy(0, pair_out, pair.at[1 - core], j, j, j).wait_recv()
+        put(sum_out, j, pair[1, j] + both * pair[0, j])
+    sum_in[chip] = sum_out[chip]
+
+    @pl.when(core == 0)
+    def _():
+        pl.semaphore_wait(barrier, 2 * (chips - 1) + 2 * (spread - 1))
+        pl.semaphore_signal(go, inc=1, device_id=(partner, col), device_id_type=MESH)
+
+    @pl.when(core == 1)
+    def _():
+        pl.semaphore_wait(go, 1)
+
+    chip_start(0, sum_out, sum_in)
+
+    doc_row = jnp.broadcast_to(docs, (tokens, tokens))
     doc_col = doc_row.T
     causal = lax.broadcasted_iota(jnp.int32, (tokens, tokens), 0) >= lax.broadcasted_iota(
         jnp.int32, (tokens, tokens), 1
@@ -131,26 +171,6 @@
     own = doc_col[:, :HD]
     first_ref[...] = jnp.where(own == own[:1], 1.0, 0.0).astype(bf16)
     last_ref[...] = jnp.where(own == own[tokens - 1 :], 1.0, 0.0).astype(bf16)
-
-    loads[0].wait()
-    loads[1].wait()
-    for j in range(half):
-        at = lanes(theirs + j)
-        pair_out[j] = dot(k_ref[:, at] * last_ref[...], v_ref[:, at], TN)
-    pl.semaphore_wait(barrier, chips + spread - 1)
-    for j in range(half):
-        core_copy(0, pair_out, pair.at[core], j, j, j).start()
-    for j in range(half):
-        at = lanes(mine + j)
-        pair[core, j] = dot(k_ref[:, at] * last_ref[...], v_ref[:, at], TN)
-
-    both = flag(sg_ref[c2] <= c0)
-    for j in range(half):
-        core_copy(0, pair_out, pair.at[1 - core], j, j, j).wait_recv()
-        put(sum_out, j, pair[1, j] + both * pair[0, j])
-    sum_in[chip] = sum_out[chip]
-    chip_start(0, sum_out, sum_in)
-
     loads[2].wait()
     loads[3].wait()
 
@@ -161,6 +181,9 @@
         weights_ref[h] = weights
         att_ref[:, at] = dot(weights, v_ref[:, at], NN)
         qf_ref[:, at] = q_ref[:, at] * first_ref[...]
+        qt_ref[h] = q_ref[:, at].T * first_row
+        kl_ref[:, at] = k_ref[:, at] * last_ref[...]
+        vl_ref[:, at] = v_ref[:, at] * last_ref[...]
         scaled_ref[:, at] = gain_ref[:, at] * g_ref[:, at].astype(f32)
         return _
 
@@ -230,7 +253,7 @@
         at = lanes(h)
         ga = (inv_ref[...] * scaled_ref[:, at] - coef_ref[...] * att_ref[:, at]).astype(bf16)
         ga_ref[:, at] = ga
-        state = dot(qf_ref[:, at], ga, TN)
+        state = dot(qt_ref[h], ga, NN)
         if i < half:
             bpair_out[j] = state
             core_copy(2, bpair_out, bpair.at[core], j, j, j).start()
@@ -280,15 +303,8 @@
     for j in range(half):
         back_in[mine + j] = (own_a * bpair[1, j] + own_b * take(brun_in, j)).astype(bf16)
 
-    for i in range(heads):
-        j = i % half
-        h = mine + j if i < half else theirs + j
-        at = lanes(h)
-        if i >= half:
-            core_copy(3, bshare_out, back_in, j, h, j).wait_recv()
-        last = last_ref[...]
-        gk_ref[:, at] = (gk_acc[:, at] + dot(v_ref[:, at] * last, back_in[h], NT)).astype(bf16)
-        gv_ref[:, at] = (gv_acc[:, at] + dot(k_ref[:, at] * last, back_in[h], NN)).astype(bf16)
+    for j in range(half):
+        core_copy(3, bshare_out, back_in, j, theirs + j, j).wait_recv()
 
     for phase, src, dst in ((0, sum_out, sum_in), (1, run_out, run_in), (2, bsum_out, bsum_in), (3, brun_out, brun_in)):
         chip_sent(phase, src, dst)
@@ -302,13 +318,28 @@
         x_copy(col, peer).wait_send()
 
 
-def write(a, b, c, d, a_out, b_out, c_out, d_out, sem):
+def finish(
+    normed_ref, gq_ref, gk_acc, gv_acc, kl_ref, vl_ref, back_ref,
+    normed_out, gq_out, gk_out, gv_out,
+    gk_ref, gv_ref, sem,
+):
+    heads = back_ref.shape[0]
     copies = [
-        pltpu.make_async_copy(src, dst, sem.at[i])
-        for i, (src, dst) in enumerate(((a, a_out), (b, b_out), (c, c_out), (d, d_out)))
+        pltpu.make_async_copy(normed_ref, normed_out, sem.at[0]),
+        pltpu.make_async_copy(gq_ref, gq_out, sem.at[1]),
     ]
     for copy in copies:
         copy.start()
+    for h in range(heads):
+        at = slice(h * HD, (h + 1) * HD)
+        gk_ref[:, at] = (gk_acc[:, at] + dot(vl_ref[:, at], back_ref[h], NT)).astype(bf16)
+        gv_ref[:, at] = (gv_acc[:, at] + dot(kl_ref[:, at], back_ref[h], NN)).astype(bf16)
+        if h % 2 == 1:
+            done = pl.ds((h - 1) * HD, 2 * HD)
+            for i, (src, dst) in enumerate(((gk_ref, gk_out), (gv_ref, gv_out))):
+                copy = pltpu.make_async_copy(src.at[:, done], dst.at[:, done], sem.at[h + 1 + i])
+                copy.start()
+                copies.append(copy)
     for copy in copies:
         copy.wait()
 
@@ -332,12 +363,12 @@
         wide_b = pltpu.VMEM((tokens, columns), bf16)
         wide_f = pltpu.VMEM((tokens, columns), f32)
         scan = [states, pair, pieces, pieces, pieces, pieces]
-        scan += [pltpu.VMEM((half, HD, HD), bf16), pltpu.VMEM((heads, HD, HD), bf16)]
+        scan += [pltpu.VMEM((half, HD, HD), bf16)]
         outs = pl.pallas_call(
             functools.partial(kernel, chips, ring, heads, spread, columns * spread),
-            out_shape=[pltpu.VMEM((tokens, columns), bf16)] * 4,
+            out_shape=[wide_b, wide_b, wide_f, wide_f, wide_b, wide_b, pltpu.VMEM((heads, HD, HD), bf16)],
             in_specs=[pl.BlockSpec(memory_space=pltpu.SMEM), vmem] + [hbm] * 4 + [vmem],
-            out_specs=[vmem] * 4,
+            out_specs=[vmem] * 7,
             scratch_shapes=[
                 *[wide_b] * 4,
                 pltpu.VMEM((tokens, tokens), f32),
@@ -349,22 +380,26 @@
                 wide_f,
                 wide_b,
                 wide_b,
-                wide_f,
-                wide_f,
+                pltpu.VMEM((heads, HD, tokens), bf16),
                 wide_f,
                 *scan,
+                pltpu.VMEM((heads, HD, HD), bf16),
                 *scan,
                 pltpu.VMEM((2, tokens), f32),
                 pltpu.VMEM((spread, 2, tokens), f32),
                 pltpu.SemaphoreType.DMA((4,)),
-                pltpu.SemaphoreType.DMA((4, chips)),
-                pltpu.SemaphoreType.DMA((4, chips)),
+                pltpu.SemaphoreType.DMA((4,)),
+                pltpu.SemaphoreType.DMA((4,)),
                 pltpu.SemaphoreType.DMA((4, half)),
                 pltpu.SemaphoreType.DMA((4, half)),
                 pltpu.SemaphoreType.DMA((spread,)),
                 pltpu.SemaphoreType.DMA((spread,)),
+                pltpu.SemaphoreType.REGULAR,
+                pltpu.SemaphoreType.REGULAR,
             ],
-            compiler_params=pltpu.CompilerParams(collective_id=0, has_side_effects=True),
+            compiler_params=pltpu.CompilerParams(
+                collective_id=0, has_side_effects=True, vmem_limit_bytes=62_300_000
+            ),
             name="attention",
         )(
             start_group,
@@ -376,13 +411,13 @@
             norm_gain.reshape(1, columns),
         )
         return pl.pallas_call(
-            write,
+            finish,
             out_shape=[jax.ShapeDtypeStruct((tokens, columns), bf16)] * 4,
-            in_specs=[vmem] * 4,
+            in_specs=[vmem] * 7,
             out_specs=[pl.BlockSpec(memory_space=pl.ANY)] * 4,
-            scratch_shapes=[pltpu.SemaphoreType.DMA((4,))],
-            compiler_params=pltpu.CompilerParams(vmem_limit_bytes=1 << 20),
-            name="write",
+            scratch_shapes=[wide_b, wide_b, pltpu.SemaphoreType.DMA((heads + 2,))],
+            compiler_params=pltpu.CompilerParams(vmem_limit_bytes=4 << 20),
+            name="finish",
         )(*outs)
 
     wide = P("seq", "head")

time: 55.1 us -> 49.1 us (0.89)
  Pallas kernels: 54.3 us -> 48.3 us
    pallas_call x1, Pallas kernels: 52.9 us -> 46.9 us  [local(): pl.pallas_call(functools.partial(kernel, chips, ring, heads, spread, colu...]
where the time goes in v4:
time: 49.1 us; the launch traced here: 48.9 us
  Pallas kernels  48.3 us (98%)
  between operations  0.64 us (1%)
    pallas_call x1, Pallas kernels, local(): pl.pallas_call(functools.partial(kernel, chips, ring, heads, spread, colu...  46.9 us
    pallas_call x1, Pallas kernels, local(): pl.pallas_call(finish, out_shape=[jax.ShapeDtypeStruct((tokens, columns),...  1.39 us

profile of v4, /device:TPU:1, one launch (start us, length us, event | category | flops | bytes accessed | tf_op | source)
XLA Modules:
  0.0 48.9 jit_solution(8157494584165123546)
XLA Ops:
  0.6 46.9 %attention.1 = (bf16[256,1024]{1,0:T(8,128)(2,1)S(1)}, bf16[256,1024]{1,0:T(8,128)(2,1)S(1)}, f32[256,1024]{1,0:T(8,128)S(1)}, f32[256,1024]{1,0:T(8,128)S(1)}, ...) custom-call(s32[64]{0:T(128)} %sg_ref.1, s32[1,256]{1,0:T(1,128)} %bitcast.3, ...), custom_call_target="tpu_custom_call" | custom-call | tf_op jit(solution)/shard_map/attention/pallas_call | solution.py:367
  47.5 1.4 %finish.1 = (bf16[256,1024]{1,0:T(8,128)(2,1)}, bf16[256,1024]{1,0:T(8,128)(2,1)}, bf16[256,1024]{1,0:T(8,128)(2,1)}, bf16[256,1024]{1,0:T(8,128)(2,1)}) custom-call(bf16[256,1024]{1,0:T(8,128)(2,1)S(1)} %get-tuple-element.11.normed_ref, bf16[256,1024]{1,0:T(8,128)(2,1)S(1)} %get-tuple-element.12.gq_ref, f32[256,1024]{1,0:T(8,128)S(1)} %get-tuple-element.13.gk_acc, ...), custom_call_target="tpu_custom_call" | custom-call | tf_op jit(solution)/shard_map/finish/pallas_call | solution.py:413

commit v5 on v4

v5 whole, which is shorter than its diff:
```python
import functools

import jax
import jax.numpy as jnp
from jax import lax
from jax.experimental import pallas as pl
from jax.experimental.pallas import tpu as pltpu
from jax.sharding import PartitionSpec as P

HD = 128
EPSILON = 1e-06
MESH = pl.DeviceIdType.MESH
f32, bf16 = jnp.float32, jnp.bfloat16


def dot(a, b, contract):
    return lax.dot_general(a, b, (contract, ((), ())), preferred_element_type=f32)


NN = ((1,), (0,))
NT = ((1,), (1,))
TN = ((0,), (0,))


def kernel(
    chips, ring, heads, spread, width,
    sg_ref, doc_ref, q_hbm, k_hbm, v_hbm, g_hbm, gain_ref,
    normed_ref, gq_ref, gk_acc, gv_acc, kl_ref, vl_ref, back_in,
    q_ref, k_ref, v_ref, g_ref, doc_in, kx_ref, vx_ref,
    same_ref, first_ref, last_ref, inv_ref, coef_ref,
    weights_ref, att_ref, ga_ref, qf_ref, qt_ref, scaled_ref,
    pair, sum_out, sum_in, run_out, run_in, carry_ref,
    bpair, bsum_out, bsum_in, brun_out, brun_in, bshare_out,
    rows_out, rows_in, normed_out, gq_out, gk_out, gv_out,
    load_sem, chip_send, chip_recv, in_send, in_recv, out_send, out_recv, core_send, core_recv,
    x_send, x_recv, here, go,
):
    seq, col = lax.axis_index("seq"), lax.axis_index("head")
    chip, core = lax.div(seq, 2), lax.rem(seq, 2)
    partner = seq + 1 - 2 * core
    tokens = q_ref.shape[1]
    half = heads // 2
    piece = sum_out.shape[1]
    pieces = HD // piece
    mine, theirs = core * half, (1 - core) * half
    c0, c1, groups = 2 * chip, 2 * chip + 1, 2 * chips
    c2 = jnp.minimum(c0 + 2, groups - 1)
    lines = chips // ring
    block = (core, 1 - core)

    def columns(first):
        return pl.ds(pl.multiple_of(first * HD, HD), half * HD)

    loads = [
        pltpu.make_async_copy(src.at[:, columns(first)], dst, load_sem.at[i])
        for i, (src, first, dst) in enumerate(
            (
                (k_hbm, mine, k_ref.at[0]),
                (v_hbm, mine, v_ref.at[0]),
                (q_hbm, mine, q_ref.at[0]),
                (g_hbm, mine, g_ref.at[0]),
                (k_hbm, theirs, kx_ref),
                (v_hbm, theirs, vx_ref),
            )
        )
    ]
    loads[0].start()
    loads[1].start()

    def hops(offset, size):
        return min(offset, size - offset)

    offsets = sorted(
        ((dz, dy) for dz in range(lines) for dy in range(ring) if dz or dy),
        key=lambda o: -(hops(o[0], lines) + hops(o[1], ring)),
    )
    chip_z, chip_y = lax.div(chip, ring), lax.rem(chip, ring)
    others = [lax.rem(chip_z + dz, lines) * ring + lax.rem(chip_y + dy, ring) for dz, dy in offsets]

    barrier = pltpu.get_barrier_semaphore()

    @pl.when(core == 0)
    def _():
        pl.semaphore_signal(barrier, inc=1, device_id=(partner, col), device_id_type=MESH)

    for other in others:
        pl.semaphore_signal(barrier, inc=1, device_id=(2 * other, col), device_id_type=MESH)
    for d in range(1, spread):
        pl.semaphore_signal(barrier, inc=1, device_id=(c0, lax.rem(col + d, spread)), device_id_type=MESH)

    def lanes(h):
        return pl.ds(pl.multiple_of(h * HD, HD), HD)

    def flag(condition):
        return jnp.where(condition, 1.0, 0.0).astype(f32)

    def to_partner(src, dst, send, recv):
        return pltpu.make_async_remote_copy(
            src_ref=src, dst_ref=dst, send_sem=send, recv_sem=recv, device_id=(partner, col), device_id_type=MESH
        )

    ins = [
        to_partner(src, dst, in_send.at[i], in_recv.at[i])
        for i, (src, dst) in enumerate(
            (
                (doc_ref, doc_in),
                (k_hbm.at[:, columns(theirs)], k_ref.at[1]),
                (v_hbm.at[:, columns(theirs)], v_ref.at[1]),
                (q_hbm.at[:, columns(theirs)], q_ref.at[1]),
                (g_hbm.at[:, columns(theirs)], g_ref.at[1]),
            )
        )
    ]
    outs = [
        to_partner(src, dst.at[:, columns(mine)], out_send.at[i], out_recv.at[i])
        for i, (src, dst) in enumerate(
            ((normed_out, normed_ref), (gq_out, gq_ref), (gk_out, gk_acc), (gv_out, gv_acc))
        )
    ]

    def close_copy(j, slot):
        return to_partner(bshare_out.at[j], back_in.at[slot], core_send.at[j], core_recv.at[j])

    def chip_copy(phase, src, dst, at_src, at_dst, other):
        return pltpu.make_async_remote_copy(
            src_ref=src.at[at_src],
            dst_ref=dst.at[at_dst],
            send_sem=chip_send.at[phase],
            recv_sem=chip_recv.at[phase],
            device_id=(2 * other + core, col),
            device_id_type=MESH,
        )

    def chip_start(phase, src, dst):
        for other in others:
            chip_copy(phase, src, dst, other, chip, other).start()

    every = pl.ds(0, chips - 1)

    def chip_wait(phase, src, dst):
        chip_copy(phase, src, dst, every, every, others[0]).wait_recv()

    def chip_sent(phase, src, dst):
        chip_copy(phase, src, dst, every, every, others[0]).wait_send()

    def put(ref, j, state):
        ref[pl.ds(j * pieces, pieces)] = state.astype(bf16).reshape(pieces, piece, HD)

    def take(ref, j):
        return ref[pl.ds(j * pieces, pieces)].reshape(HD, HD).astype(f32)

    @pl.when(core == 1)
    def _():
        pl.semaphore_wait(barrier, 1)
        pl.semaphore_signal(here, inc=1, device_id=(partner, col), device_id_type=MESH)

    @pl.when(core == 0)
    def _():
        pl.semaphore_wait(here, 1)

    for copy in ins:
        copy.start()
    for load in loads[2:]:
        load.start()

    def edges(ids):
        docs = ids.astype(f32)
        return (
            docs,
            jnp.where(docs == docs[:, :1], 1.0, 0.0).astype(bf16),
            jnp.where(docs == docs[:, tokens - 1 :], 1.0, 0.0).astype(bf16),
        )

    def tails(role, last_row):
        for j in range(half):
            at = lanes(j)
            pair[block[role], j] = dot(k_ref[role, :, at].T * last_row, v_ref[role, :, at], NN)

    marks = [edges(doc_ref[...]), None]
    loads[0].wait()
    loads[1].wait()
    tails(0, marks[0][2])
    for copy in ins[:3]:
        copy.wait_recv()
    marks[1] = edges(doc_in[...])
    tails(1, marks[1][2])

    both = flag(sg_ref[c2] <= c0)
    for j in range(half):
        put(sum_out, j, pair[1, j] + both * pair[0, j])
    sum_in[chip] = sum_out[chip]

    @pl.when(core == 0)
    def _():
        pl.semaphore_wait(barrier, 2 * (chips - 1) + 2 * (spread - 1))
        pl.semaphore_signal(go, inc=1, device_id=(partner, col), device_id_type=MESH)

    @pl.when(core == 1)
    def _():
        pl.semaphore_wait(go, 1)

    chip_start(0, sum_out, sum_in)

    causal = lax.broadcasted_iota(jnp.int32, (tokens, tokens), 0) >= lax.broadcasted_iota(
        jnp.int32, (tokens, tokens), 1
    )
    for role in range(2):
        doc_row = jnp.broadcast_to(marks[role][0], (tokens, tokens))
        doc_col = doc_row.T
        same_ref[role] = jnp.where(causal & (doc_row == doc_col), 1.0, 0.0)
        own = doc_col[:, :HD]
        first_ref[role] = jnp.where(own == own[:1], 1.0, 0.0).astype(bf16)
        if role == 0:
            last_ref[...] = jnp.where(own == own[tokens - 1 :], 1.0, 0.0).astype(bf16)
    for load in loads[2:]:
        load.wait()
    for copy in ins[3:]:
        copy.wait_recv()

    for role in range(2):

        def local_forward(j, _, role=role):
            at = lanes(j)
            query = q_ref[role, :, at]
            scores = dot(query, k_ref[role, :, at], NT)
            weights = jnp.where(same_ref[role] > 0.5, scores, 0.0).astype(bf16)
            weights_ref[role, j] = weights
            att_ref[role, :, at] = dot(weights, v_ref[role, :, at], NN)
            qf_ref[role, :, at] = query * first_ref[role]
            qt_ref[role, j] = query.T * marks[role][1]
            scaled_ref[role, :, at] = gain_ref[:, lanes(mine + j)] * g_ref[role, :, at].astype(f32)
            if role == 0:
                kl_ref[:, lanes(mine + j)] = k_ref[0, :, at] * last_ref[...]
                vl_ref[:, lanes(mine + j)] = v_ref[0, :, at] * last_ref[...]
                kl_ref[:, lanes(theirs + j)] = kx_ref[:, at] * last_ref[...]
                vl_ref[:, lanes(theirs + j)] = vx_ref[:, at] * last_ref[...]
            return _

        lax.fori_loop(0, half, local_forward, 0)

    chip_wait(0, sum_out, sum_in)
    run = jnp.zeros((piece, HD), f32)
    run_out[0] = run.astype(bf16)
    for w in range(1, chips):
        begin = sg_ref[2 * w]
        run = flag(begin <= 2 * w - 1) * (sum_in[w - 1].astype(f32) + flag(begin < 2 * w - 2) * run)
        run_out[w] = run.astype(bf16)
    run_in[chip] = run_out[chip]
    chip_start(1, run_out, run_in)
    chip_wait(1, run_out, run_in)

    odd = core == 1
    inside, through = flag(sg_ref[c1] <= c0), flag(sg_ref[c1] < c0)
    own_a, own_b = jnp.where(odd, inside, 0.0), jnp.where(odd, through, 1.0)
    their_a, their_b = jnp.where(odd, 0.0, inside), jnp.where(odd, 1.0, through)
    for j in range(half):
        state, entering = pair[0, j], take(run_in, j)
        carry_ref[0, j] = (own_a * state + own_b * entering).astype(bf16)
        carry_ref[1, j] = (their_a * state + their_b * entering).astype(bf16)

    for role in range(2):
        square = jnp.zeros((tokens, HD), f32)
        cross = jnp.zeros((tokens, HD), f32)
        for j in range(half):
            at = lanes(j)
            att = att_ref[role, :, at] + dot(qf_ref[role, :, at], carry_ref[role, j], NN)
            att_ref[role, :, at] = att
            square = square + att * att
            cross = cross + scaled_ref[role, :, at] * att
        rows_out[block[role], 0:1] = jnp.sum(square.T, axis=0, keepdims=True)
        rows_out[block[role], 1:2] = jnp.sum(cross.T, axis=0, keepdims=True)

    own_slot = 2 * col + core

    def x_copy(slot, peer):
        return pltpu.make_async_remote_copy(
            src_ref=rows_out,
            dst_ref=rows_in.at[slot],
            send_sem=x_send.at[peer],
            recv_sem=x_recv.at[slot],
            device_id=(c0 + lax.rem(peer, 2), lax.div(peer, 2)),
            device_id_type=MESH,
        )

    peers = [
        2 * lax.rem(col + d, spread) + lax.rem(core + e, 2)
        for d in sorted(range(spread), key=lambda d: -hops(d, spread))
        for e in range(2)
        if d or e
    ]
    for peer in peers:
        x_copy(own_slot, peer).start()
    sums = rows_out[...]
    for peer in reversed(peers):
        x_copy(peer, peer).wait_recv()
        sums = sums + rows_in[peer]
    rows_out_sum = sums
    inverse = lax.rsqrt(rows_out_sum[:, 0:1] / width + EPSILON)
    coef = inverse * inverse * inverse * rows_out_sum[:, 1:2] / width
    for b in range(2):
        at_role = jnp.where(core == b, 0, 1)
        inv_ref[at_role] = jnp.broadcast_to(inverse[b], (HD, tokens)).T
        coef_ref[at_role] = jnp.broadcast_to(coef[b], (HD, tokens)).T

    for role in range(2):
        for j in range(half):
            at = lanes(j)
            ga = inv_ref[role] * scaled_ref[role, :, at] - coef_ref[role] * att_ref[role, :, at]
            ga = ga.astype(bf16)
            ga_ref[role, :, at] = ga
            bpair[block[role], j] = dot(qt_ref[role, j], ga, NN)

    from_first, from_second = flag(sg_ref[c0] < c0), flag(sg_ref[c1] < c0)
    for j in range(half):
        put(bsum_out, j, from_first * bpair[0, j] + from_second * bpair[1, j])
    bsum_in[chip] = bsum_out[chip]
    chip_start(2, bsum_out, bsum_in)

    def local_backward(role, to_normed, to_gq, to_gk, to_gv, first):
        def one(j, _):
            at = lanes(j)
            to = lanes(first + j)
            ga = ga_ref[role, :, at]
            normed = att_ref[role, :, at] * inv_ref[role] * gain_ref[:, lanes(mine + j)]
            to_normed[:, to] = normed.astype(bf16)
            scores = dot(ga, v_ref[role, :, at], NT)
            scores = jnp.where(same_ref[role] > 0.5, scores, 0.0).astype(bf16)
            part = dot(ga * first_ref[role], carry_ref[role, j], NT)
            to_gq[:, to] = (dot(scores, k_ref[role, :, at], NN) + part).astype(bf16)
            to_gk[:, to] = dot(scores, q_ref[role, :, at], TN)
            to_gv[:, to] = dot(weights_ref[role, j], ga, TN)
            return _

        lax.fori_loop(0, half, one, 0)

    local_backward(1, normed_out, gq_out, gk_out, gv_out, 0)
    for copy in outs:
        copy.start()

    chip_wait(2, bsum_out, bsum_in)
    run = jnp.zeros((piece, HD), f32)
    brun_out[chips - 1] = run.astype(bf16)
    for w in range(chips - 2, -1, -1):
        run = flag(sg_ref[min(2 * w + 4, groups - 1)] <= 2 * w + 1) * run
        run = flag(sg_ref[2 * w + 2] <= 2 * w + 1) * (bsum_in[w + 1].astype(f32) + run)
        brun_out[w] = run.astype(bf16)
    brun_in[chip] = brun_out[chip]
    chip_start(3, brun_out, brun_in)

    local_backward(0, normed_ref, gq_ref, gk_acc, gv_acc, mine)

    chip_wait(3, brun_out, brun_in)
    reach = flag(sg_ref[c2] <= c0)
    own_a, own_b = jnp.where(odd, 0.0, inside), jnp.where(odd, 1.0, reach)
    their_a, their_b = jnp.where(odd, inside, 0.0), jnp.where(odd, reach, 1.0)
    for j in range(half):
        bshare_out[j] = (their_a * bpair[1, j] + their_b * take(brun_in, j)).astype(bf16)
        close_copy(j, mine + j).start()
    for j in range(half):
        back_in[mine + j] = (own_a * bpair[1, j] + own_b * take(brun_in, j)).astype(bf16)

    for j in range(half):
        close_copy(j, theirs + j).wait_recv()

    for phase, src, dst in ((0, sum_out, sum_in), (1, run_out, run_in), (2, bsum_out, bsum_in), (3, brun_out, brun_in)):
        chip_sent(phase, src, dst)
    for copy in ins:
        copy.wait_send()
    for copy in outs:
        copy.wait_send()
        copy.wait_recv()
    for j in range(half):
        close_copy(j, mine + j).wait_send()
    for peer in peers:
        x_copy(own_slot, peer).wait_send()


def finish(
    normed_ref, gq_ref, gk_acc, gv_acc, kl_ref, vl_ref, back_ref,
    normed_out, gq_out, gk_out, gv_out,
    gk_ref, gv_ref, sem,
):
    heads = back_ref.shape[0]
    copies = [
        pltpu.make_async_copy(normed_ref, normed_out, sem.at[0]),
        pltpu.make_async_copy(gq_ref, gq_out, sem.at[1]),
    ]
    for copy in copies:
        copy.start()
    for h in range(heads):
        at = slice(h * HD, (h + 1) * HD)
        gk_ref[:, at] = (gk_acc[:, at] + dot(vl_ref[:, at], back_ref[h], NT)).astype(bf16)
        gv_ref[:, at] = (gv_acc[:, at] + dot(kl_ref[:, at], back_ref[h], NN)).astype(bf16)
        if h % 2 == 1:
            done = pl.ds((h - 1) * HD, 2 * HD)
            for i, (src, dst) in enumerate(((gk_ref, gk_out), (gv_ref, gv_out))):
                copy = pltpu.make_async_copy(src.at[:, done], dst.at[:, done], sem.at[h + 1 + i])
                copy.start()
                copies.append(copy)
    for copy in copies:
        copy.wait()


def solution(mesh):
    groups, spread = mesh.shape["seq"], mesh.shape["head"]
    chips = groups // 2
    ring = 4 if chips % 4 == 0 else 1

    def local(query_in, key_in, value_in, out_grad, norm_gain, doc_ids, start_group):
        tokens, columns = query_in.shape
        heads = columns // HD
        half = heads // 2
        vmem = pl.BlockSpec(memory_space=pltpu.VMEM)
        hbm = pl.BlockSpec(memory_space=pltpu.HBM)
        pair = pltpu.VMEM((2, half, HD, HD), f32)
        pieces = pltpu.VMEM((chips, half * HD // chips, HD), bf16)
        closed = pltpu.VMEM((half, HD, HD), bf16)
        narrow = pltpu.VMEM((2, tokens, HD), bf16)
        row = pltpu.VMEM((2, tokens, HD), f32)
        wide_b = pltpu.VMEM((tokens, columns), bf16)
        wide_f = pltpu.VMEM((tokens, columns), f32)
        half_b = pltpu.VMEM((tokens, columns // 2), bf16)
        half_f = pltpu.VMEM((tokens, columns // 2), f32)
        both_b = pltpu.VMEM((2, tokens, columns // 2), bf16)
        both_f = pltpu.VMEM((2, tokens, columns // 2), f32)
        dma = pltpu.SemaphoreType.DMA
        outs = pl.pallas_call(
            functools.partial(kernel, chips, ring, heads, spread, columns * spread),
            out_shape=[wide_b, wide_b, wide_f, wide_f, wide_b, wide_b, pltpu.VMEM((heads, HD, HD), bf16)],
            in_specs=[pl.BlockSpec(memory_space=pltpu.SMEM), vmem] + [hbm] * 4 + [vmem],
            out_specs=[vmem] * 7,
            scratch_shapes=[
                *[both_b] * 4,
                pltpu.VMEM((1, tokens), jnp.int32),
                half_b,
                half_b,
                pltpu.VMEM((2, tokens, tokens), f32),
                narrow,
                pltpu.VMEM((tokens, HD), bf16),
                row,
                row,
                pltpu.VMEM((2, half, tokens, tokens), bf16),
                both_f,
                both_b,
                both_b,
                pltpu.VMEM((2, half, HD, tokens), bf16),
                both_f,
                *[pair, pieces, pieces, pieces, pieces],
                pltpu.VMEM((2, half, HD, HD), bf16),
                *[pair, pieces, pieces, pieces, pieces],
                closed,
                pltpu.VMEM((2, 2, tokens), f32),
                pltpu.VMEM((2 * spread, 2, 2, tokens), f32),
                half_b,
                half_b,
                half_f,
                half_f,
                dma((6,)),
                dma((4,)),
                dma((4,)),
                dma((5,)),
                dma((5,)),
                dma((4,)),
                dma((4,)),
                dma((half,)),
                dma((half,)),
                dma((2 * spread,)),
                dma((2 * spread,)),
                pltpu.SemaphoreType.REGULAR,
                pltpu.SemaphoreType.REGULAR,
            ],
            compiler_params=pltpu.CompilerParams(
                collective_id=0, has_side_effects=True, vmem_limit_bytes=62_300_000
            ),
            name="attention",
        )(
            start_group,
            doc_ids.reshape(1, tokens),
            query_in,
            key_in,
            value_in,
            out_grad,
            norm_gain.reshape(1, columns),
        )
        return pl.pallas_call(
            finish,
            out_shape=[jax.ShapeDtypeStruct((tokens, columns), bf16)] * 4,
            in_specs=[vmem] * 7,
            out_specs=[pl.BlockSpec(memory_space=pl.ANY)] * 4,
            scratch_shapes=[wide_b, wide_b, pltpu.SemaphoreType.DMA((heads + 2,))],
            compiler_params=pltpu.CompilerParams(vmem_limit_bytes=4 << 20),
            name="finish",
        )(*outs)

    wide = P("seq", "head")
    return jax.shard_map(
        local,
        mesh=mesh,
        in_specs=(wide, wide, wide, wide, P("head"), P("seq"), P()),
        out_specs=(wide, wide, wide, wide),
        check_vma=False,
    )
```

time: 49.1 us -> 46.9 us (0.955)
  Pallas kernels: 48.3 us -> 46.1 us
    pallas_call x1, Pallas kernels: 46.9 us -> 44.7 us  [local(): pl.pallas_call(functools.partial(kernel, chips, ring, heads, spread, colu...]
where the time goes in v5:
time: 46.9 us; the launch traced here: 46.7 us
  Pallas kernels  46.1 us (98%)
  between operations  0.64 us (1%)
    pallas_call x1, Pallas kernels, local(): pl.pallas_call(functools.partial(kernel, chips, ring, heads, spread, colu...  44.7 us
    pallas_call x1, Pallas kernels, local(): pl.pallas_call(finish, out_shape=[jax.ShapeDtypeStruct((tokens, columns),...  1.39 us

profile of v5, /device:TPU:1, one launch (start us, length us, event | category | flops | bytes accessed | tf_op | source)
XLA Modules:
  0.0 46.7 jit_solution(12466043733953951309)
XLA Ops:
  0.6 44.7 %attention.1 = (bf16[256,1024]{1,0:T(8,128)(2,1)S(1)}, bf16[256,1024]{1,0:T(8,128)(2,1)S(1)}, f32[256,1024]{1,0:T(8,128)S(1)}, f32[256,1024]{1,0:T(8,128)S(1)}, ...) custom-call(s32[64]{0:T(128)} %sg_ref.1, s32[1,256]{1,0:T(1,128)} %bitcast.3, ...), custom_call_target="tpu_custom_call" | custom-call | tf_op jit(solution)/shard_map/attention/pallas_call | solution.py:427
  45.3 1.4 %finish.1 = (bf16[256,1024]{1,0:T(8,128)(2,1)}, bf16[256,1024]{1,0:T(8,128)(2,1)}, bf16[256,1024]{1,0:T(8,128)(2,1)}, bf16[256,1024]{1,0:T(8,128)(2,1)}) custom-call(bf16[256,1024]{1,0:T(8,128)(2,1)S(1)} %get-tuple-element.11.normed_ref, bf16[256,1024]{1,0:T(8,128)(2,1)S(1)} %get-tuple-element.12.gq_ref, f32[256,1024]{1,0:T(8,128)S(1)} %get-tuple-element.13.gk_acc, ...), custom_call_target="tpu_custom_call" | custom-call | tf_op jit(solution)/shard_map/finish/pallas_call | solution.py:485

commit v6 on v5

--- a/solution.py
+++ b/solution.py
@@ -24,9 +24,9 @@
 
 def kernel(
     chips, ring, heads, spread, width,
-    sg_ref, doc_ref, q_hbm, k_hbm, v_hbm, g_hbm, gain_ref,
+    sg_hbm, doc_hbm, q_hbm, k_hbm, v_hbm, g_hbm, gain_hbm,
     normed_ref, gq_ref, gk_acc, gv_acc, kl_ref, vl_ref, back_in,
-    q_ref, k_ref, v_ref, g_ref, doc_in, kx_ref, vx_ref,
+    sg_ref, doc_ref, gain_ref, q_ref, k_ref, v_ref, g_ref, doc_in, kx_ref, vx_ref,
     same_ref, first_ref, last_ref, inv_ref, coef_ref,
     weights_ref, att_ref, ga_ref, qf_ref, qt_ref, scaled_ref,
     pair, sum_out, sum_in, run_out, run_in, carry_ref,
@@ -64,8 +64,10 @@
             )
         )
     ]
-    loads[0].start()
-    loads[1].start()
+    smalls = [
+        pltpu.make_async_copy(src, dst, load_sem.at[len(loads) + i])
+        for i, (src, dst) in enumerate(((doc_hbm, doc_ref), (sg_hbm, sg_ref), (gain_hbm, gain_ref)))
+    ]
 
     def hops(offset, size):
         return min(offset, size - offset)
@@ -88,6 +90,9 @@
     for d in range(1, spread):
         pl.semaphore_signal(barrier, inc=1, device_id=(c0, lax.rem(col + d, spread)), device_id_type=MESH)
 
+    for copy in smalls[:2] + loads[:2] + smalls[2:]:
+        copy.start()
+
     def lanes(h):
         return pl.ds(pl.multiple_of(h * HD, HD), HD)
 
@@ -103,7 +108,7 @@
         to_partner(src, dst, in_send.at[i], in_recv.at[i])
         for i, (src, dst) in enumerate(
             (
-                (doc_ref, doc_in),
+                (doc_hbm, doc_in),
                 (k_hbm.at[:, columns(theirs)], k_ref.at[1]),
                 (v_hbm.at[:, columns(theirs)], v_ref.at[1]),
                 (q_hbm.at[:, columns(theirs)], q_ref.at[1]),
@@ -176,6 +181,7 @@
             at = lanes(j)
             pair[block[role], j] = dot(k_ref[role, :, at].T * last_row, v_ref[role, :, at], NN)
 
+    smalls[0].wait()
     marks = [edges(doc_ref[...]), None]
     loads[0].wait()
     loads[1].wait()
@@ -185,6 +191,7 @@
     marks[1] = edges(doc_in[...])
     tails(1, marks[1][2])
 
+    smalls[1].wait()
     both = flag(sg_ref[c2] <= c0)
     for j in range(half):
         put(sum_out, j, pair[1, j] + both * pair[0, j])
@@ -212,6 +219,7 @@
         first_ref[role] = jnp.where(own == own[:1], 1.0, 0.0).astype(bf16)
         if role == 0:
             last_ref[...] = jnp.where(own == own[tokens - 1 :], 1.0, 0.0).astype(bf16)
+    smalls[2].wait()
     for load in loads[2:]:
         load.wait()
     for copy in ins[3:]:
@@ -239,12 +247,29 @@
         lax.fori_loop(0, half, local_forward, 0)
 
     chip_wait(0, sum_out, sum_in)
-    run = jnp.zeros((piece, HD), f32)
-    run_out[0] = run.astype(bf16)
-    for w in range(1, chips):
-        begin = sg_ref[2 * w]
-        run = flag(begin <= 2 * w - 1) * (sum_in[w - 1].astype(f32) + flag(begin < 2 * w - 2) * run)
-        run_out[w] = run.astype(bf16)
+    inner = [[jnp.zeros((piece, HD), f32)] for _ in range(lines)]
+    for i in range(1, ring + 1):
+        for line in range(lines):
+            w = line * ring + i
+            if w < chips:
+                begin = sg_ref[2 * w]
+                value = sum_in[w - 1].astype(f32)
+                if i > 1:
+                    value = value + flag(begin < 2 * w - 2) * inner[line][-1]
+                inner[line].append(flag(begin <= 2 * w - 1) * value)
+    run = None
+    for line in range(lines):
+        for i in range(ring):
+            w = line * ring + i
+            value = inner[line][i]
+            if line > 0:
+                value = value + flag(sg_ref[2 * w] < 2 * line * ring) * run
+            run_out[w] = value.astype(bf16)
+        if line + 1 < lines:
+            value = inner[line][ring]
+            if line > 0:
+                value = value + flag(sg_ref[2 * (line + 1) * ring] < 2 * line * ring) * run
+            run = value
     run_in[chip] = run_out[chip]
     chip_start(1, run_out, run_in)
     chip_wait(1, run_out, run_in)
@@ -338,12 +363,32 @@
         copy.start()
 
     chip_wait(2, bsum_out, bsum_in)
-    run = jnp.zeros((piece, HD), f32)
-    brun_out[chips - 1] = run.astype(bf16)
-    for w in range(chips - 2, -1, -1):
-        run = flag(sg_ref[min(2 * w + 4, groups - 1)] <= 2 * w + 1) * run
-        run = flag(sg_ref[2 * w + 2] <= 2 * w + 1) * (bsum_in[w + 1].astype(f32) + run)
-        brun_out[w] = run.astype(bf16)
+    inner = [[None] * ring for _ in range(lines)]
+    for i in range(ring - 1, -1, -1):
+        for line in range(lines):
+            w = line * ring + i
+            if i == ring - 1:
+                inner[line][i] = jnp.zeros((piece, HD), f32)
+            else:
+                value = bsum_in[w + 1].astype(f32)
+                if i < ring - 2:
+                    value = value + flag(sg_ref[2 * w + 4] <= 2 * w + 1) * inner[line][i + 1]
+                inner[line][i] = flag(sg_ref[2 * w + 2] <= 2 * w + 1) * value
+    run = None
+    for line in range(lines - 1, -1, -1):
+        behind = (line + 1) * ring
+        for i in range(ring - 1, -1, -1):
+            w = line * ring + i
+            value = inner[line][i]
+            if line + 1 < lines:
+                value = value + flag(sg_ref[2 * behind] <= 2 * w + 1) * run
+            brun_out[w] = value.astype(bf16)
+        if line > 0:
+            w = line * ring
+            value = bsum_in[w].astype(f32) + flag(sg_ref[2 * w + 2] <= 2 * w - 1) * inner[line][0]
+            if line + 1 < lines:
+                value = value + flag(sg_ref[2 * behind] <= 2 * w - 1) * run
+            run = value
     brun_in[chip] = brun_out[chip]
     chip_start(3, brun_out, brun_in)
 
@@ -427,9 +472,12 @@
         outs = pl.pallas_call(
             functools.partial(kernel, chips, ring, heads, spread, columns * spread),
             out_shape=[wide_b, wide_b, wide_f, wide_f, wide_b, wide_b, pltpu.VMEM((heads, HD, HD), bf16)],
-            in_specs=[pl.BlockSpec(memory_space=pltpu.SMEM), vmem] + [hbm] * 4 + [vmem],
+            in_specs=[hbm] * 7,
             out_specs=[vmem] * 7,
             scratch_shapes=[
+                pltpu.SMEM((groups,), jnp.int32),
+                pltpu.VMEM((1, tokens), jnp.int32),
+                pltpu.VMEM((1, columns), f32),
                 *[both_b] * 4,
                 pltpu.VMEM((1, tokens), jnp.int32),
                 half_b,
@@ -455,7 +503,7 @@
                 half_b,
                 half_f,
                 half_f,
-                dma((6,)),
+                dma((9,)),
                 dma((4,)),
                 dma((4,)),
                 dma((5,)),

time: 46.9 us -> 46.1 us (0.983)
  Pallas kernels: 46.1 us -> 45.4 us
    pallas_call x1, Pallas kernels: 44.7 us -> 44 us  [local(): pl.pallas_call(functools.partial(kernel, chips, ring, heads, spread, colu...]
where the time goes in v6:
time: 46.1 us; the launch traced here: 46 us
  Pallas kernels  45.4 us (98%)
  between operations  0.64 us (1%)
    pallas_call x1, Pallas kernels, local(): pl.pallas_call(functools.partial(kernel, chips, ring, heads, spread, colu...  44 us
    pallas_call x1, Pallas kernels, local(): pl.pallas_call(finish, out_shape=[jax.ShapeDtypeStruct((tokens, columns),...  1.39 us

profile of v6, /device:TPU:1, one launch (start us, length us, event | category | flops | bytes accessed | tf_op | source)
XLA Modules:
  0.0 46.0 jit_solution(8705191913863522990)
XLA Ops:
  0.6 44.0 %attention.1 = (bf16[256,1024]{1,0:T(8,128)(2,1)S(1)}, bf16[256,1024]{1,0:T(8,128)(2,1)S(1)}, f32[256,1024]{1,0:T(8,128)S(1)}, f32[256,1024]{1,0:T(8,128)S(1)}, ...) custom-call(s32[64]{0:T(128)} %sg_hbm.1, s32[1,256]{1,0:T(1,128)} %bitcast.3, ...), custom_call_target="tpu_custom_call" | custom-call | tf_op jit(solution)/shard_map/attention/pallas_call | solution.py:472
  44.6 1.4 %finish.1 = (bf16[256,1024]{1,0:T(8,128)(2,1)}, bf16[256,1024]{1,0:T(8,128)(2,1)}, bf16[256,1024]{1,0:T(8,128)(2,1)}, bf16[256,1024]{1,0:T(8,128)(2,1)}) custom-call(bf16[256,1024]{1,0:T(8,128)(2,1)S(1)} %get-tuple-element.11.normed_ref, bf16[256,1024]{1,0:T(8,128)(2,1)S(1)} %get-tuple-element.12.gq_ref, f32[256,1024]{1,0:T(8,128)S(1)} %get-tuple-element.13.gk_acc, ...), custom_call_target="tpu_custom_call" | custom-call | tf_op jit(solution)/shard_map/finish/pallas_call | solution.py:533

commit v7 on v6

--- a/solution.py
+++ b/solution.py
@@ -74,10 +74,13 @@
 
     offsets = sorted(
         ((dz, dy) for dz in range(lines) for dy in range(ring) if dz or dy),
-        key=lambda o: -(hops(o[0], lines) + hops(o[1], ring)),
+        key=lambda o: (-(hops(o[0], lines) + hops(o[1], ring)), -hops(o[1], ring), o),
     )
     chip_z, chip_y = lax.div(chip, ring), lax.rem(chip, ring)
-    others = [lax.rem(chip_z + dz, lines) * ring + lax.rem(chip_y + dy, ring) for dz, dy in offsets]
+    turn = 1 - 2 * core
+    at_z = [lax.rem(chip_z + lines + turn * dz, lines) * ring for dz in range(lines)]
+    at_y = [lax.rem(chip_y + ring + turn * dy, ring) for dy in range(ring)]
+    others = [at_z[dz] + at_y[dy] for dz, dy in offsets]
 
     barrier = pltpu.get_barrier_semaphore()
 

time: 46.1 us -> 46 us (level)
  no operation moved by 1% of the time
where the time goes in v7:
time: 46 us; the launch traced here: 45.9 us
  Pallas kernels  45.2 us (98%)
  between operations  0.64 us (1%)
    pallas_call x1, Pallas kernels, local(): pl.pallas_call(functools.partial(kernel, chips, ring, heads, spread, colu...  43.8 us
    pallas_call x1, Pallas kernels, local(): pl.pallas_call(finish, out_shape=[jax.ShapeDtypeStruct((tokens, columns),...  1.39 us

profile of v7, /device:TPU:1, one launch (start us, length us, event | category | flops | bytes accessed | tf_op | source)
XLA Modules:
  0.0 45.9 jit_solution(148977544840807221)
XLA Ops:
  0.6 43.8 %attention.1 = (bf16[256,1024]{1,0:T(8,128)(2,1)S(1)}, bf16[256,1024]{1,0:T(8,128)(2,1)S(1)}, f32[256,1024]{1,0:T(8,128)S(1)}, f32[256,1024]{1,0:T(8,128)S(1)}, ...) custom-call(s32[64]{0:T(128)} %sg_hbm.1, s32[1,256]{1,0:T(1,128)} %bitcast.3, ...), custom_call_target="tpu_custom_call" | custom-call | tf_op jit(solution)/shard_map/attention/pallas_call | solution.py:475
  44.5 1.4 %finish.1 = (bf16[256,1024]{1,0:T(8,128)(2,1)}, bf16[256,1024]{1,0:T(8,128)(2,1)}, bf16[256,1024]{1,0:T(8,128)(2,1)}, bf16[256,1024]{1,0:T(8,128)(2,1)}) custom-call(bf16[256,1024]{1,0:T(8,128)(2,1)S(1)} %get-tuple-element.11.normed_ref, bf16[256,1024]{1,0:T(8,128)(2,1)S(1)} %get-tuple-element.12.gq_ref, f32[256,1024]{1,0:T(8,128)S(1)} %get-tuple-element.13.gk_acc, ...), custom_call_target="tpu_custom_call" | custom-call | tf_op jit(solution)/shard_map/finish/pallas_call | solution.py:536

commit v8 on v7

--- a/solution.py
+++ b/solution.py
@@ -249,24 +249,26 @@
 
         lax.fori_loop(0, half, local_forward, 0)
 
+    joins = [flag(sg_ref[2 * w] <= 2 * w - 1) for w in range(1, chips)]
+    keeps = [flag(sg_ref[2 * w] < 2 * w - 2) for w in range(1, chips)]
+    enters = [flag(sg_ref[2 * w] < 2 * (w // ring) * ring) for w in range(chips)]
     chip_wait(0, sum_out, sum_in)
     inner = [[jnp.zeros((piece, HD), f32)] for _ in range(lines)]
     for i in range(1, ring + 1):
         for line in range(lines):
             w = line * ring + i
             if w < chips:
-                begin = sg_ref[2 * w]
                 value = sum_in[w - 1].astype(f32)
                 if i > 1:
-                    value = value + flag(begin < 2 * w - 2) * inner[line][-1]
-                inner[line].append(flag(begin <= 2 * w - 1) * value)
+                    value = value + keeps[w - 1] * inner[line][-1]
+                inner[line].append(joins[w - 1] * value)
     run = None
     for line in range(lines):
         for i in range(ring):
             w = line * ring + i
             value = inner[line][i]
             if line > 0:
-                value = value + flag(sg_ref[2 * w] < 2 * line * ring) * run
+                value = value + enters[w] * run
             run_out[w] = value.astype(bf16)
         if line + 1 < lines:
             value = inner[line][ring]
@@ -286,6 +288,13 @@
         carry_ref[0, j] = (own_a * state + own_b * entering).astype(bf16)
         carry_ref[1, j] = (their_a * state + their_b * entering).astype(bf16)
 
+    ones = jnp.ones((16, HD), bf16)
+
+    def across(x):
+        high = x.astype(bf16)
+        low = (x - high.astype(f32)).astype(bf16)
+        return (dot(ones, high, NT) + dot(ones, low, NT))[0:1]
+
     for role in range(2):
         square = jnp.zeros((tokens, HD), f32)
         cross = jnp.zeros((tokens, HD), f32)
@@ -295,8 +304,8 @@
             att_ref[role, :, at] = att
             square = square + att * att
             cross = cross + scaled_ref[role, :, at] * att
-        rows_out[block[role], 0:1] = jnp.sum(square.T, axis=0, keepdims=True)
-        rows_out[block[role], 1:2] = jnp.sum(cross.T, axis=0, keepdims=True)
+        rows_out[block[role], 0:1] = across(square)
+        rows_out[block[role], 1:2] = across(cross)
 
     own_slot = 2 * col + core
 
@@ -322,13 +331,16 @@
     for peer in reversed(peers):
         x_copy(peer, peer).wait_recv()
         sums = sums + rows_in[peer]
-    rows_out_sum = sums
-    inverse = lax.rsqrt(rows_out_sum[:, 0:1] / width + EPSILON)
-    coef = inverse * inverse * inverse * rows_out_sum[:, 1:2] / width
-    for b in range(2):
-        at_role = jnp.where(core == b, 0, 1)
-        inv_ref[at_role] = jnp.broadcast_to(inverse[b], (HD, tokens)).T
-        coef_ref[at_role] = jnp.broadcast_to(coef[b], (HD, tokens)).T
+    inverse = lax.rsqrt(sums[:, 0:1] / width + EPSILON)
+    coef = inverse * inverse * inverse * sums[:, 1:2] / width
+    first_role = flag(core == 0)
+    scales = [
+        first_role * part[role] + (1.0 - first_role) * part[1 - role] for role in range(2) for part in (inverse, coef)
+    ]
+    by_token = jnp.concatenate(scales + scales, axis=0).T
+    for role in range(2):
+        inv_ref[role] = jnp.broadcast_to(by_token[:, 2 * role : 2 * role + 1], (tokens, HD))
+        coef_ref[role] = jnp.broadcast_to(by_token[:, 2 * role + 1 : 2 * role + 2], (tokens, HD))
 
     for role in range(2):
         for j in range(half):

time: 46 us -> 46.4 us (level)
  no operation moved by 1% of the time
where the time goes in v8:
time: 46.4 us; the launch traced here: 46.3 us
  Pallas kernels  45.6 us (98%)
  between operations  0.64 us (1%)
    pallas_call x1, Pallas kernels, local(): pl.pallas_call(functools.partial(kernel, chips, ring, heads, spread, colu...  44.2 us
    pallas_call x1, Pallas kernels, local(): pl.pallas_call(finish, out_shape=[jax.ShapeDtypeStruct((tokens, columns),...  1.39 us

profile of v8, /device:TPU:1, one launch (start us, length us, event | category | flops | bytes accessed | tf_op | source)
XLA Modules:
  0.0 46.3 jit_solution(12754127061675295467)
XLA Ops:
  0.6 44.2 %attention.1 = (bf16[256,1024]{1,0:T(8,128)(2,1)S(1)}, bf16[256,1024]{1,0:T(8,128)(2,1)S(1)}, f32[256,1024]{1,0:T(8,128)S(1)}, f32[256,1024]{1,0:T(8,128)S(1)}, ...) custom-call(s32[64]{0:T(128)} %sg_hbm.1, s32[1,256]{1,0:T(1,128)} %bitcast.3, ...), custom_call_target="tpu_custom_call" | custom-call | tf_op jit(solution)/shard_map/attention/pallas_call | solution.py:487
  44.9 1.4 %finish.1 = (bf16[256,1024]{1,0:T(8,128)(2,1)}, bf16[256,1024]{1,0:T(8,128)(2,1)}, bf16[256,1024]{1,0:T(8,128)(2,1)}, bf16[256,1024]{1,0:T(8,128)(2,1)}) custom-call(bf16[256,1024]{1,0:T(8,128)(2,1)S(1)} %get-tuple-element.11.normed_ref, bf16[256,1024]{1,0:T(8,128)(2,1)S(1)} %get-tuple-element.12.gq_ref, f32[256,1024]{1,0:T(8,128)S(1)} %get-tuple-element.13.gk_acc, ...), custom_call_target="tpu_custom_call" | custom-call | tf_op jit(solution)/shard_map/finish/pallas_call | solution.py:548
